TPU v7x, 32 devices: a whole 2x2x4 slice. The times are simulated.
32 devices in a mesh: row: 16 (over z, y, core), col: 2 (over x).
Axes of the slice: x: 2, y: 2, z: 4, core: 2. Of those that a mesh axis runs over, the one named last changes fastest.
Arguments:
- specimen_slices: float32 [2, 2, 4096, 512], P(None, None, 'row', 'col'), may hold values from -6 to 6
- illumination_probe: float32 [2, 128, 128], replicated, may hold values from -6 to 6
- propagation_phase: float32 [128, 128], replicated, may hold values from -3.140625 to 3.140625
- amplitudes: float32 [16, 2, 4, 128, 128], P('row', 'col'), may hold values from 0.5 to 4
- positions: int32 [16, 2, 4, 2], P('row', 'col'), may hold values from 0 to 255
- counts: int32 [16, 2], P('row', 'col'), may hold values from 1 to 4, as said below
- measurement_index: int32 [16, 2, 4], P('row', 'col'), may hold values from 0 to 3, each once within a row
Outputs:
- updated: float32 [2, 2, 4096, 512], P(None, None, 'row', 'col')
Inputs may be any that keep to these rules, and one draw needn't show every extreme that they name: `counts`: some tile holds exactly 4 probe positions.
All inputs are finite; a program needn't handle non-finite values.
Results may differ from a plain program's by a relative error of at most 0.0001.
Values sent between devices are 32-bit elements; how exact they have to be, the bound alone decides.
No kernel may reach another device: no remote copies, remote signals or barrier semaphores. Data moves between devices by JAX's collectives and lax.ppermute only.
A program may use at most 64 MiB of HBM per device.

v0:
```python
import functools
import math

import jax
import jax.numpy as jnp
import ml_dtypes
import numpy as np
from jax import lax
from jax.experimental import pallas as pl
from jax.experimental.pallas import tpu as pltpu
from jax.sharding import PartitionSpec as P

ITERS = 2
LANES = 128

step_size = 0.02
floor_amp = 0.5


def from_behind(block, axis, distance):
    devices = range(lax.axis_size(axis))
    route = [((i - distance) % len(devices), i) for i in devices]
    return lax.ppermute(block, axis, route)


def two_parts(value):
    high = value.astype(ml_dtypes.bfloat16)
    low = (value - high.astype(np.float64)).astype(ml_dtypes.bfloat16)
    return high, low


def dft_operands(width):
    index = np.arange(width)
    angle = (index[:, None] * index[None, :] % width) * (2.0 * math.pi / width)
    real = np.cos(angle) / math.sqrt(width)
    imag = -np.sin(angle) / math.sqrt(width)
    right = np.block([[real, imag], [-imag, real]])
    right_high, right_low = two_parts(right)
    left_high, left_low = two_parts(right.T)
    return (
        np.concatenate([right_high, right_high], 0),
        right_low,
        np.concatenate([left_high, left_high], 1),
        left_low,
    )


def split(value):
    high = value.astype(jnp.bfloat16)
    low = (value - high.astype(jnp.float32)).astype(jnp.bfloat16)
    return high, low


def rows_of(j, width):
    return slice(j * width, (j + 1) * width)


def put(a_ref, j, width, real, imag):
    real_high, real_low = split(real)
    imag_high, imag_low = split(imag)
    rows = rows_of(j, width)
    a_ref[rows, 0:width] = real_high
    a_ref[rows, width:2 * width] = imag_high
    a_ref[rows, 2 * width:3 * width] = real_low
    a_ref[rows, 3 * width:4 * width] = imag_low


def transform(a_ref, b_ref, tables, spots, width):
    right_high_ref, right_low_ref, left_high_ref, left_low_ref = tables
    half = jnp.dot(a_ref[...], right_high_ref[...], preferred_element_type=jnp.float32)
    half += jnp.dot(a_ref[:, :2 * width], right_low_ref[...], preferred_element_type=jnp.float32)
    for j in range(spots):
        rows = rows_of(j, width)
        real_high, real_low = split(half[rows, :width])
        imag_high, imag_low = split(half[rows, width:])
        b_ref[0:width, rows] = real_high
        b_ref[width:2 * width, rows] = imag_high
        b_ref[2 * width:3 * width, rows] = real_low
        b_ref[3 * width:4 * width, rows] = imag_low
    full = jnp.dot(left_high_ref[...], b_ref[...], preferred_element_type=jnp.float32)
    full += jnp.dot(left_low_ref[...], b_ref[:2 * width, :], preferred_element_type=jnp.float32)
    return [
        (full[:width, rows_of(j, width)], full[width:, rows_of(j, width)]) for j in range(spots)
    ]


def fill_ext(ext_ref, tile_ref, below_ref, upper_ref, lower_ref, corner_ref, width):
    tile_px = tile_ref.shape[1]
    blocks = tile_px // LANES
    for c in range(2):
        for b in range(blocks):
            lanes = slice(b * LANES, (b + 1) * LANES)
            ext_ref[c, b, :tile_px, :] = tile_ref[c, :, lanes]
            ext_ref[c, b, tile_px:, :] = below_ref[c, :, lanes]
        ext_ref[c, blocks, :width, :] = upper_ref[c]
        ext_ref[c, blocks, width:tile_px, :] = lower_ref[c]
        ext_ref[c, blocks, tile_px:, :] = corner_ref[c]


def place(pos_ref, j):
    col = pos_ref[2 * j + 1]
    return pos_ref[2 * j], col // LANES, col % LANES


def window(ext_ref, c, spot, width, lane):
    row, block, shift = spot
    near = ext_ref[c, block, pl.ds(row, width), :]
    far = ext_ref[c, block + 1, pl.ds(row, width), :]
    return pltpu.roll(jnp.where(lane >= shift, near, far), LANES - shift, 1)


def scatter(grad_ref, c, spot, width, lane, used, update):
    row, block, shift = spot
    turned = pltpu.roll(jnp.where(used, update, 0.0), shift, 1)
    near = lane >= shift
    grad_ref[c, block, pl.ds(row, width), :] += jnp.where(near, turned, 0.0)
    grad_ref[c, block + 1, pl.ds(row, width), :] += jnp.where(near, 0.0, turned)


def emit(grad_ref, own_ref, down_ref, upper_ref, lower_ref, diag_ref, width):
    tile_px = own_ref.shape[1]
    blocks = tile_px // LANES
    for c in range(2):
        for b in range(blocks):
            lanes = slice(b * LANES, (b + 1) * LANES)
            own_ref[c, :, lanes] = grad_ref[c, b, :tile_px, :]
            down_ref[c, :, lanes] = grad_ref[c, b, tile_px:, :]
        upper_ref[c] = grad_ref[c, blocks, :width, :]
        lower_ref[c] = grad_ref[c, blocks, width:tile_px, :]
        diag_ref[c] = grad_ref[c, blocks, tile_px:, :]


def lanes_of(width):
    return lax.broadcasted_iota(jnp.int32, (width, LANES), 1)


def forward_kernel(
    pos_ref, tile_ref, below_ref, upper_ref, lower_ref, corner_ref, probe_ref, prop_ref,
    rh_ref, rl_ref, lh_ref, ll_ref, moved_ref, ext_ref, a_ref, b_ref, *, spots, width,
):
    tables = (rh_ref, rl_ref, lh_ref, ll_ref)
    fill_ext(ext_ref, tile_ref, below_ref, upper_ref, lower_ref, corner_ref, width)
    lane = lanes_of(width)
    for j in range(spots):
        spot = place(pos_ref, j)
        real = window(ext_ref, 0, spot, width, lane)
        imag = window(ext_ref, 1, spot, width, lane)
        put(
            a_ref, j, width,
            probe_ref[0] * real - probe_ref[1] * imag,
            probe_ref[0] * imag + probe_ref[1] * real,
        )
    for j, (real, imag) in enumerate(transform(a_ref, b_ref, tables, spots, width)):
        put(
            a_ref, j, width,
            prop_ref[0] * real - prop_ref[1] * imag,
            -(prop_ref[0] * imag + prop_ref[1] * real),
        )
    for j, (real, negative) in enumerate(transform(a_ref, b_ref, tables, spots, width)):
        moved_ref[j, 0] = real
        moved_ref[j, 1] = -negative


def middle_kernel(
    pos_ref, count_ref, slot_ref, tile_ref, below_ref, upper_ref, lower_ref, corner_ref,
    moved_ref, amp_ref, rh_ref, rl_ref, lh_ref, ll_ref,
    own_ref, down_ref, up_out_ref, low_out_ref, diag_ref, back_ref,
    ext_ref, win_ref, a_ref, b_ref, *, spots, width,
):
    tables = (rh_ref, rl_ref, lh_ref, ll_ref)
    fill_ext(ext_ref, tile_ref, below_ref, upper_ref, lower_ref, corner_ref, width)
    lane = lanes_of(width)
    total = count_ref[0]
    spot_list = [place(pos_ref, j) for j in range(spots)]
    for j in range(spots):
        second_real = window(ext_ref, 0, spot_list[j], width, lane)
        second_imag = window(ext_ref, 1, spot_list[j], width, lane)
        win_ref[j, 0] = second_real
        win_ref[j, 1] = second_imag
        put(
            a_ref, j, width,
            moved_ref[j, 0] * second_real - moved_ref[j, 1] * second_imag,
            moved_ref[j, 0] * second_imag + moved_ref[j, 1] * second_real,
        )
    ext_ref[...] = jnp.zeros(ext_ref.shape, jnp.float32)
    for j, (real, imag) in enumerate(transform(a_ref, b_ref, tables, spots, width)):
        measured = amp_ref[slot_ref[j]]
        power = jnp.maximum(real * real + imag * imag, floor_amp * floor_amp)
        factor = 1.0 - measured * lax.rsqrt(power)
        put(a_ref, j, width, real * factor, -(imag * factor))
    for j, (real, negative) in enumerate(transform(a_ref, b_ref, tables, spots, width)):
        imag = -negative
        used = j < total
        scatter(ext_ref, 0, spot_list[j], width, lane, used, moved_ref[j, 0] * real + moved_ref[j, 1] * imag)
        scatter(ext_ref, 1, spot_list[j], width, lane, used, moved_ref[j, 0] * imag - moved_ref[j, 1] * real)
        back_ref[j, 0] = win_ref[j, 0] * real + win_ref[j, 1] * imag
        back_ref[j, 1] = win_ref[j, 0] * imag - win_ref[j, 1] * real
    emit(ext_ref, own_ref, down_ref, up_out_ref, low_out_ref, diag_ref, width)


def backward_kernel(
    pos_ref, count_ref, back_ref, probe_ref, prop_ref, rh_ref, rl_ref, lh_ref, ll_ref,
    own_ref, down_ref, up_out_ref, low_out_ref, diag_ref,
    ext_ref, a_ref, b_ref, *, spots, width,
):
    tables = (rh_ref, rl_ref, lh_ref, ll_ref)
    lane = lanes_of(width)
    total = count_ref[0]
    for j in range(spots):
        put(a_ref, j, width, back_ref[j, 0], back_ref[j, 1])
    ext_ref[...] = jnp.zeros(ext_ref.shape, jnp.float32)
    for j, (real, imag) in enumerate(transform(a_ref, b_ref, tables, spots, width)):
        put(
            a_ref, j, width,
            prop_ref[0] * real + prop_ref[1] * imag,
            -(prop_ref[0] * imag - prop_ref[1] * real),
        )
    for j, (real, negative) in enumerate(transform(a_ref, b_ref, tables, spots, width)):
        imag = -negative
        spot = place(pos_ref, j)
        used = j < total
        scatter(ext_ref, 0, spot, width, lane, used, probe_ref[0] * real + probe_ref[1] * imag)
        scatter(ext_ref, 1, spot, width, lane, used, probe_ref[0] * imag - probe_ref[1] * real)
    emit(ext_ref, own_ref, down_ref, up_out_ref, low_out_ref, diag_ref, width)


def folded(tile_ref, own_ref, above_ref, upper_ref, lower_ref, c, width):
    tile_px = own_ref.shape[1]
    top, low = slice(0, width), slice(width, tile_px)
    left, rest = slice(0, width), slice(width, tile_px)
    yield top, left, tile_ref[c, top, left] - step_size * (
        own_ref[c, top, left] + above_ref[c, :, left] + upper_ref[c]
    )
    yield top, rest, tile_ref[c, top, rest] - step_size * (own_ref[c, top, rest] + above_ref[c, :, rest])
    yield low, left, tile_ref[c, low, left] - step_size * (own_ref[c, low, left] + lower_ref[c])
    yield low, rest, tile_ref[c, low, rest] - step_size * own_ref[c, low, rest]


def update_kernel(
    tile_ref, own_ref, above_ref, upper_ref, lower_ref,
    new_ref, top_ref, left_up_ref, left_low_ref, *, width,
):
    for c in range(2):
        for k, (rows, lanes, value) in enumerate(
            folded(tile_ref, own_ref, above_ref, upper_ref, lower_ref, c, width)
        ):
            new_ref[c, rows, lanes] = value
            if k < 2:
                top_ref[c, :, lanes] = value
            if k == 0:
                left_up_ref[c] = value
            if k == 2:
                left_low_ref[c] = value


def finish_kernel(*refs, width):
    out_ref = refs[-1]
    for s in range(2):
        for c in range(2):
            for rows, lanes, value in folded(*refs[5 * s:5 * s + 5], c, width):
                out_ref[s, c, rows, lanes] = value


F32 = functools.partial(jax.ShapeDtypeStruct, dtype=jnp.float32)
SMEM = pl.BlockSpec(memory_space=pltpu.SMEM)
VMEM = pl.BlockSpec(memory_space=pltpu.VMEM)
LIMIT = pltpu.CompilerParams(vmem_limit_bytes=16 * 1024 * 1024)


def call(kernel, scalars, arrays, outs, scratch, name, **static):
    return pl.pallas_call(
        functools.partial(kernel, **static),
        in_specs=[SMEM] * len(scalars) + [VMEM] * len(arrays),
        out_specs=[VMEM] * len(outs),
        out_shape=outs,
        scratch_shapes=scratch,
        compiler_params=LIMIT,
        name=name,
    )(*scalars, *arrays)


def body(
    specimen_slices,
    illumination_probe,
    propagation_phase,
    amplitudes,
    positions,
    counts,
    measurement_index,
):
    tile_px = specimen_slices.shape[2]
    width = illumination_probe.shape[1]
    spots = positions.shape[2]
    ext = tile_px + width
    tables = [jnp.asarray(t) for t in dft_operands(width)]
    prop = jnp.stack([jnp.cos(propagation_phase), jnp.sin(propagation_phase)])
    where = positions.reshape(-1)
    count = counts.reshape(-1)
    slots = measurement_index.reshape(-1)
    measured = amplitudes[0, 0]
    static = dict(spots=spots, width=width)
    ext_space = pltpu.VMEM((2, ext // LANES, ext, LANES), jnp.float32)
    work = [
        pltpu.VMEM((spots * width, 4 * width), jnp.bfloat16),
        pltpu.VMEM((4 * width, spots * width), jnp.bfloat16),
    ]
    wave = F32((spots, 2, width, width))
    square = F32((2, width, width))
    whole = F32((2, tile_px, tile_px))
    strip = F32((2, width, tile_px))
    gradient = [whole, strip, square, square, square]

    def halo(top, left_up, left_low):
        upper = from_behind(left_up, "col", -1)
        lower = from_behind(left_low, "col", -1)
        below = from_behind(top, "row", -1)
        corner = from_behind(upper, "row", -1)
        return below, upper, lower, corner

    def fold(own, down, side_up, side_low, diag):
        corner = from_behind(diag, "row", 1)
        lower = from_behind(side_low, "col", 1)
        above = from_behind(down, "row", 1)
        upper = from_behind(side_up + corner, "col", 1)
        return own, above, upper, lower

    tiles = [specimen_slices[0], specimen_slices[1]]
    sends = [(t[:, :width, :], t[:, :width, :width], t[:, width:, :width]) for t in tiles]
    for iteration in range(ITERS):
        halo_one = halo(*sends[0])
        halo_two = halo(*sends[1])
        (moved,) = call(
            forward_kernel, (where,), (tiles[0], *halo_one, illumination_probe, prop, *tables),
            [wave], [ext_space, *work], "forward_wave", **static,
        )
        *grad_two, back = call(
            middle_kernel, (where, count, slots), (tiles[1], *halo_two, moved, measured, *tables),
            [*gradient, wave], [ext_space, pltpu.VMEM((spots, 2, width, width), jnp.float32), *work],
            "residual_wave", **static,
        )
        fold_two = fold(*grad_two)
        grad_one = call(
            backward_kernel, (where, count), (back, illumination_probe, prop, *tables),
            gradient, [ext_space, *work], "backward_wave", **static,
        )
        fold_one = fold(*grad_one)
        if iteration + 1 < ITERS:
            fresh, sends = [], []
            for tile, received in zip(tiles, (fold_one, fold_two)):
                new, *send = call(
                    update_kernel, (), (tile, *received), [whole, strip, square, square], [],
                    "update_slice", width=width,
                )
                fresh.append(new)
                sends.append(send)
            tiles = fresh
        else:
            (updated,) = call(
                finish_kernel, (), (tiles[0], *fold_one, tiles[1], *fold_two),
                [F32(specimen_slices.shape)], [], "finish", width=width,
            )
    return updated


def solution(mesh):
    placed = (
        P(None, None, "row", "col"),
        P(),
        P(),
        P("row", "col", None, None, None),
        P("row", "col", None, None),
        P("row", "col"),
        P("row", "col", None),
    )
    return jax.shard_map(
        body, mesh=mesh, in_specs=placed, out_specs=P(None, None, "row", "col"), check_vma=False
    )
```

profile of v0, /device:TPU:0, one launch (start us, length us, event | category | flops | bytes accessed | tf_op | source)
XLA Modules:
  0.0 82.9 jit_solution(8466604546473883301)
XLA Ops:
  0.0 1.3 %slice_bitcast_fusion = (f32[2,256,256]{2,1,0:T(8,128)S(1)}, f32[2,256,256]{2,1,0:T(8,128)S(1)}) fusion(f32[2,2,256,256]{3,2,1,0:T(8,128)} %param.11), kind=kLoop, calls=%fused_computation | loop fusion | bytes 2097152 | tf_op jit(solution)/shard_map/squeeze | solution.py:327
  1.9 3.0 %collective-permute-start.1 = (f32[2,128,128]{2,1,0:T(8,128)S(1)}, f32[2,128,128]{2,1,0:T(8,128)S(1)}, u32[]{:S(2)}, u32[]{:S(2)}) collective-permute-start(f32[2,128,128]{2,1,0:T(8,128)S(1)} %get-tuple-element.70), channel_id=1, source_target_pairs={{1,0},{0,1},{3,2},{2,3},{5,4},{4,5},{7,6},{6,7},{9,8},{8,9},{11,10... | collective-permute-start | bytes 393224 | tf_op jit(solution)/shard_map/ppermute | solution.py:23
  5.0 2.0 %collective-permute-start.5 = (f32[2,128,128]{2,1,0:T(8,128)S(1)}, f32[2,128,128]{2,1,0:T(8,128)S(1)}, u32[]{:S(2)}, u32[]{:S(2)}) collective-permute-start(f32[2,128,128]{2,1,0:T(8,128)S(1)} %get-tuple-element.68), channel_id=1, source_target_pairs={{1,0},{0,1},{3,2},{2,3},{5,4},{4,5},{7,6},{6,7},{9,8},{8,9},{11,10... | collective-permute-start | bytes 393224 | tf_op jit(solution)/shard_map/ppermute | solution.py:23
  7.8 3.3 %collective-permute-start.4 = (f32[2,128,256]{2,1,0:T(8,128)}, f32[2,128,256]{2,1,0:T(8,128)S(1)}, u32[]{:S(2)}, u32[]{:S(2)}) collective-permute-start(f32[2,128,256]{2,1,0:T(8,128)} %slice.35), channel_id=1, source_target_pairs={{2,0},{4,2},{6,4},{8,6},{10,8},{12,10},{14,12},{16,14},{18,16},{20... | collective-permute-start | bytes 786440 | tf_op jit(solution)/shard_map/ppermute | solution.py:23
  11.2 1.8 %collective-permute-start = (f32[2,128,256]{2,1,0:T(8,128)S(1)}, f32[2,128,256]{2,1,0:T(8,128)S(1)}, u32[]{:S(2)}, u32[]{:S(2)}) collective-permute-start(f32[2,128,256]{2,1,0:T(8,128)S(1)} %slice.32), channel_id=1, source_target_pairs={{2,0},{4,2},{6,4},{8,6},{10,8},{12,10},{14,12},{16,14},{18,16},{20... | collective-permute-start | bytes 786440 | tf_op jit(solution)/shard_map/ppermute | solution.py:23
  13.1 1.5 %collective-permute-start.3 = (f32[2,128,128]{2,1,0:T(8,128)S(1)}, f32[2,128,128]{2,1,0:T(8,128)S(1)}, u32[]{:S(2)}, u32[]{:S(2)}) collective-permute-start(f32[2,128,128]{2,1,0:T(8,128)S(1)} %collective-permute-done.1.upper_ref), channel_id=1, source_target_pairs={{2,0},{4,2},{6,4},{8,6},{10,8},{12,10},{14,12},{16,14},{18,16},{20... | collective-permute-start | bytes 393224 | tf_op jit(solution)/shard_map/ppermute | solution.py:23
  14.9 2.5 %collective-permute-start.7 = (f32[2,128,128]{2,1,0:T(8,128)S(1)}, f32[2,128,128]{2,1,0:T(8,128)S(1)}, u32[]{:S(2)}, u32[]{:S(2)}) collective-permute-start(f32[2,128,128]{2,1,0:T(8,128)S(1)} %collective-permute-done.5.upper_ref), channel_id=1, source_target_pairs={{2,0},{4,2},{6,4},{8,6},{10,8},{12,10},{14,12},{16,14},{18,16},{20... | collective-permute-start | bytes 393224 | tf_op jit(solution)/shard_map/ppermute | solution.py:23
  18.5 2.3 %collective-permute-done.7.corner_ref = f32[2,128,128]{2,1,0:T(8,128)S(1)} collective-permute-done((f32[2,128,128]{2,1,0:T(8,128)S(1)}, f32[2,128,128]{2,1,0:T(8,128)S(1)}, u32[]{:S(2)}, u32[]{:S(2)}) %collective-permute-start.7) | collective-permute-done | bytes 131104 | tf_op jit(solution)/shard_map/ppermute | solution.py:23
  20.9 2.8 %forward_wave.2.moved_ref = f32[4,2,128,128]{3,2,1,0:T(8,128)S(1)} custom-call(s32[8]{0:T(128)S(1)} %reshape.9.pos_ref, f32[2,256,256]{2,1,0:T(8,128)S(1)} %get-tuple-element.66.tile_ref, f32[2,128,256]{2,1,0:T(8,128)S(1)} %collective-permute-done.4.below_ref, f32[2,128,128]{2,1,0:T(8,128)S(1)} %collective-permute-done.5.upper_ref, ...), custom_call_target="tpu_custom_call" | custom-call | tf_op jit(solution)/shard_map/forward_wave/pallas_call | solution.py:271
  24.4 3.1 %residual_wave.2 = (f32[2,256,256]{2,1,0:T(8,128)S(1)}, f32[2,128,256]{2,1,0:T(8,128)S(1)}, f32[2,128,128]{2,1,0:T(8,128)S(1)}, f32[2,128,128]{2,1,0:T(8,128)S(1...) custom-call(s32[8]{0:T(128)S(1)} %reshape.9.pos_ref, s32[1]{0:T(128)} %bitcast.11.count_ref, ...), custom_call_target="tpu_custom_call" | custom-call | tf_op jit(solution)/shard_map/residual_wave/pallas_call | solution.py:271
  27.5 2.9 %backward_wave.2 = (f32[2,256,256]{2,1,0:T(8,128)S(1)}, f32[2,128,256]{2,1,0:T(8,128)S(1)}, f32[2,128,128]{2,1,0:T(8,128)S(1)}, f32[2,128,128]{2,1,0:T(8,128)S(1)}, f32[2,128,128]{2,1,0:T(8,128)S(1)}) custom-call(s32[8]{0:T(128)S(1)} %reshape.9.pos_ref, s32[1]{0:T(128)} %bitcast.12.count_ref, f32[4,2,128,128]{3,2,1,0:T(8,128)S(1)} %get-tuple-element.35.back_ref, ...), custom_call_target="tpu_custom_call" | custom-call | tf_op jit(solution)/shard_map/backward_wave/pallas_call | solution.py:271
  31.0 1.5 %collective-permute-start.11 = (f32[2,128,128]{2,1,0:T(8,128)S(1)}, f32[2,128,128]{2,1,0:T(8,128)S(1)}, u32[]{:S(2)}, u32[]{:S(2)}) collective-permute-start(f32[2,128,128]{2,1,0:T(8,128)S(1)} %get-tuple-element.40), channel_id=1, source_target_pairs={{1,0},{0,1},{3,2},{2,3},{5,4},{4,5},{7,6},{6,7},{9,8},{8,9},{11,10... | collective-permute-start | bytes 393224 | tf_op jit(solution)/shard_map/ppermute | solution.py:23
  32.5 5.2 %collective-permute-done.9 = f32[2,128,128]{2,1,0:T(8,128)S(1)} collective-permute-done((f32[2,128,128]{2,1,0:T(8,128)S(1)}, f32[2,128,128]{2,1,0:T(8,128)S(1)}, u32[]{:S(2)}, u32[]{:S(2)}) %collective-permute-start.9) | collective-permute-done | bytes 131104 | tf_op jit(solution)/shard_map/ppermute | solution.py:23
  37.7 1.6 %collective-permute-start.10 = (f32[2,128,128]{2,1,0:T(8,128)S(1)}, f32[2,128,128]{2,1,0:T(8,128)S(1)}, u32[]{:S(2)}, u32[]{:S(2)}) collective-permute-start(f32[2,128,128]{2,1,0:T(8,128)S(1)} %add.12), channel_id=1, source_target_pairs={{1,0},{0,1},{3,2},{2,3},{5,4},{4,5},{7,6},{6,7},{9,8},{8,9},{11,10... | collective-permute-start | bytes 393224 | tf_op jit(solution)/shard_map/ppermute | solution.py:23
  39.3 2.6 %collective-permute-done.13 = f32[2,128,128]{2,1,0:T(8,128)S(1)} collective-permute-done((f32[2,128,128]{2,1,0:T(8,128)S(1)}, f32[2,128,128]{2,1,0:T(8,128)S(1)}, u32[]{:S(2)}, u32[]{:S(2)}) %collective-permute-start.13) | collective-permute-done | bytes 131104 | tf_op jit(solution)/shard_map/ppermute | solution.py:23
  41.9 1.5 %collective-permute-start.15 = (f32[2,128,128]{2,1,0:T(8,128)S(1)}, f32[2,128,128]{2,1,0:T(8,128)S(1)}, u32[]{:S(2)}, u32[]{:S(2)}) collective-permute-start(f32[2,128,128]{2,1,0:T(8,128)S(1)} %get-tuple-element.46), channel_id=1, source_target_pairs={{1,0},{0,1},{3,2},{2,3},{5,4},{4,5},{7,6},{6,7},{9,8},{8,9},{11,10... | collective-permute-start | bytes 393224 | tf_op jit(solution)/shard_map/ppermute | solution.py:23
  44.2 1.6 %collective-permute-start.21 = (f32[2,128,128]{2,1,0:T(8,128)S(1)}, f32[2,128,128]{2,1,0:T(8,128)S(1)}, u32[]{:S(2)}, u32[]{:S(2)}) collective-permute-start(f32[2,128,128]{2,1,0:T(8,128)S(1)} %get-tuple-element.52), channel_id=1, source_target_pairs={{1,0},{0,1},{3,2},{2,3},{5,4},{4,5},{7,6},{6,7},{9,8},{8,9},{11,10... | collective-permute-start | bytes 393224 | tf_op jit(solution)/shard_map/ppermute | solution.py:23
  46.9 1.6 %collective-permute-done.14.upper_ref = f32[2,128,128]{2,1,0:T(8,128)S(1)} collective-permute-done((f32[2,128,128]{2,1,0:T(8,128)S(1)}, f32[2,128,128]{2,1,0:T(8,128)S(1)}, u32[]{:S(2)}, u32[]{:S(2)}) %collective-permute-start.14) | collective-permute-done | bytes 131104 | tf_op jit(solution)/shard_map/ppermute | solution.py:23
  48.6 1.6 %collective-permute-start.17 = (f32[2,128,128]{2,1,0:T(8,128)S(1)}, f32[2,128,128]{2,1,0:T(8,128)S(1)}, u32[]{:S(2)}, u32[]{:S(2)}) collective-permute-start(f32[2,128,128]{2,1,0:T(8,128)S(1)} %get-tuple-element.49), channel_id=1, source_target_pairs={{1,0},{0,1},{3,2},{2,3},{5,4},{4,5},{7,6},{6,7},{9,8},{8,9},{11,10... | collective-permute-start | bytes 393224 | tf_op jit(solution)/shard_map/ppermute | solution.py:23
  50.8 3.1 %collective-permute-start.23 = (f32[2,128,128]{2,1,0:T(8,128)S(1)}, f32[2,128,128]{2,1,0:T(8,128)S(1)}, u32[]{:S(2)}, u32[]{:S(2)}) collective-permute-start(f32[2,128,128]{2,1,0:T(8,128)S(1)} %collective-permute-done.21.upper_ref), channel_id=1, source_target_pairs={{2,0},{4,2},{6,4},{8,6},{10,8},{12,10},{14,12},{16,14},{18,16},{20... | collective-permute-start | bytes 393224 | tf_op jit(solution)/shard_map/ppermute | solution.py:23
  54.1 2.5 %collective-permute-start.18 = (f32[2,128,128]{2,1,0:T(8,128)S(1)}, f32[2,128,128]{2,1,0:T(8,128)S(1)}, u32[]{:S(2)}, u32[]{:S(2)}) collective-permute-start(f32[2,128,128]{2,1,0:T(8,128)S(1)} %get-tuple-element.50), channel_id=1, source_target_pairs={{1,0},{0,1},{3,2},{2,3},{5,4},{4,5},{7,6},{6,7},{9,8},{8,9},{11,10... | collective-permute-start | bytes 393224 | tf_op jit(solution)/shard_map/ppermute | solution.py:23
  56.9 2.2 %collective-permute-start.19 = (f32[2,128,128]{2,1,0:T(8,128)S(1)}, f32[2,128,128]{2,1,0:T(8,128)S(1)}, u32[]{:S(2)}, u32[]{:S(2)}) collective-permute-start(f32[2,128,128]{2,1,0:T(8,128)S(1)} %collective-permute-done.17.upper_ref), channel_id=1, source_target_pairs={{2,0},{4,2},{6,4},{8,6},{10,8},{12,10},{14,12},{16,14},{18,16},{20... | collective-permute-start | bytes 393224 | tf_op jit(solution)/shard_map/ppermute | solution.py:23
  59.1 2.8 %forward_wave.3.moved_ref = f32[4,2,128,128]{3,2,1,0:T(8,128)S(1)} custom-call(s32[8]{0:T(128)S(1)} %reshape.9.pos_ref, f32[2,256,256]{2,1,0:T(8,128)S(1)} %get-tuple-element.41.tile_ref.refs_0_, f32[2,128,256]{2,1,0:T(8,128)S(1)} %collective-permute-done.20.below_ref, f32[2,128,128]{2,1,0:T(8,128)S(1)} %collective-permute-done.21.upper_ref, ...), custom_call_target="tpu_custom_call" | custom-call | tf_op jit(solution)/shard_map/forward_wave/pallas_call | solution.py:271
  61.9 3.1 %residual_wave.3 = (f32[2,256,256]{2,1,0:T(8,128)S(1)}, f32[2,128,256]{2,1,0:T(8,128)S(1)}, f32[2,128,128]{2,1,0:T(8,128)S(1)}, f32[2,128,128]{2,1,0:T(8,128)S(1...) custom-call(s32[8]{0:T(128)S(1)} %reshape.9.pos_ref, s32[1]{0:T(128)} %bitcast.13.count_ref, ...), custom_call_target="tpu_custom_call" | custom-call | tf_op jit(solution)/shard_map/residual_wave/pallas_call | solution.py:271
  65.2 2.9 %backward_wave.3 = (f32[2,256,256]{2,1,0:T(8,128)S(1)}, f32[2,128,256]{2,1,0:T(8,128)S(1)}, f32[2,128,128]{2,1,0:T(8,128)S(1)}, f32[2,128,128]{2,1,0:T(8,128)S(1)}, f32[2,128,128]{2,1,0:T(8,128)S(1)}) custom-call(s32[8]{0:T(128)S(1)} %reshape.9.pos_ref, s32[1]{0:T(128)} %bitcast.14.count_ref, f32[4,2,128,128]{3,2,1,0:T(8,128)S(1)} %get-tuple-element.54.back_ref, ...), custom_call_target="tpu_custom_call" | custom-call | tf_op jit(solution)/shard_map/backward_wave/pallas_call | solution.py:271
  69.8 2.5 %collective-permute-done.29 = f32[2,128,128]{2,1,0:T(8,128)S(1)} collective-permute-done((f32[2,128,128]{2,1,0:T(8,128)S(1)}, f32[2,128,128]{2,1,0:T(8,128)S(1)}, u32[]{:S(2)}, u32[]{:S(2)}) %collective-permute-start.29) | collective-permute-done | bytes 131104 | tf_op jit(solution)/shard_map/ppermute | solution.py:23
  72.9 2.4 %collective-permute-done.25 = f32[2,128,128]{2,1,0:T(8,128)S(1)} collective-permute-done((f32[2,128,128]{2,1,0:T(8,128)S(1)}, f32[2,128,128]{2,1,0:T(8,128)S(1)}, u32[]{:S(2)}, u32[]{:S(2)}) %collective-permute-start.25) | collective-permute-done | bytes 131104 | tf_op jit(solution)/shard_map/ppermute | solution.py:23
  76.1 1.3 %collective-permute-start.26 = (f32[2,128,128]{2,1,0:T(8,128)S(1)}, f32[2,128,128]{2,1,0:T(8,128)S(1)}, u32[]{:S(2)}, u32[]{:S(2)}) collective-permute-start(f32[2,128,128]{2,1,0:T(8,128)S(1)} %add.14), channel_id=1, source_target_pairs={{1,0},{0,1},{3,2},{2,3},{5,4},{4,5},{7,6},{6,7},{9,8},{8,9},{11,10... | collective-permute-start | bytes 393224 | tf_op jit(solution)/shard_map/ppermute | solution.py:23
  77.4 1.3 %collective-permute-done.27.refs_4_ = f32[2,128,128]{2,1,0:T(8,128)S(1)} collective-permute-done((f32[2,128,128]{2,1,0:T(8,128)S(1)}, f32[2,128,128]{2,1,0:T(8,128)S(1)}, u32[]{:S(2)}, u32[]{:S(2)}) %collective-permute-start.27) | collective-permute-done | bytes 131104 | tf_op jit(solution)/shard_map/ppermute | solution.py:23
  78.7 1.6 %collective-permute-done.30.refs_8_ = f32[2,128,128]{2,1,0:T(8,128)S(1)} collective-permute-done((f32[2,128,128]{2,1,0:T(8,128)S(1)}, f32[2,128,128]{2,1,0:T(8,128)S(1)}, u32[]{:S(2)}, u32[]{:S(2)}) %collective-permute-start.30) | collective-permute-done | bytes 131104 | tf_op jit(solution)/shard_map/ppermute | solution.py:23
  80.3 1.4 %collective-permute-done.26.refs_3_ = f32[2,128,128]{2,1,0:T(8,128)S(1)} collective-permute-done((f32[2,128,128]{2,1,0:T(8,128)S(1)}, f32[2,128,128]{2,1,0:T(8,128)S(1)}, u32[]{:S(2)}, u32[]{:S(2)}) %collective-permute-start.26) | collective-permute-done | bytes 131104 | tf_op jit(solution)/shard_map/ppermute | solution.py:23
  81.7 1.2 %finish.1 = f32[2,2,256,256]{3,2,1,0:T(8,128)} custom-call(f32[2,256,256]{2,1,0:T(8,128)S(1)} %get-tuple-element.41.tile_ref.refs_0_, f32[2,256,256]{2,1,0:T(8,128)S(1)} %get-tuple-element.55.refs_1_, f32[2,128,256]{2,1,0:T(8,128)S(1)} %collective-permute-done.24.refs_2_, f32[2,128,128]{2,1,0:T(8,128)S(1)} %collective-permute-done.26.refs_3_, ...), custom_call_target="tpu_custom_call" | custom-call | tf_op jit(solution)/shard_map/finish/pallas_call | solution.py:271
  (72 shorter events, 10.0 us)
Async XLA Ops:
  1.9 9.3 %collective-permute-start.1 = (f32[2,128,128]{2,1,0:T(8,128)S(1)}, f32[2,128,128]{2,1,0:T(8,128)S(1)}, u32[]{:S(2)}, u32[]{:S(2)}) collective-permute-start(f32[2,128,128]{2,1,0:T(8,128)S(1)} %get-tuple-element.70), channel_id=1, source_target_pairs={{1,0},{0,1},{3,2},{2,3},{5,4},{4,5},{7,6},{6,7},{9,8},{8,9},{11,10... | collective-permute-start | bytes 393224 | tf_op jit(solution)/shard_map/ppermute | solution.py:23
  4.9 8.1 %collective-permute-start.6 = (f32[2,128,128]{2,1,0:T(8,128)S(1)}, f32[2,128,128]{2,1,0:T(8,128)S(1)}, u32[]{:S(2)}, u32[]{:S(2)}) collective-permute-start(f32[2,128,128]{2,1,0:T(8,128)S(1)} %get-tuple-element.67), channel_id=1, source_target_pairs={{1,0},{0,1},{3,2},{2,3},{5,4},{4,5},{7,6},{6,7},{9,8},{8,9},{11,10... | collective-permute-start | bytes 393224 | tf_op jit(solution)/shard_map/ppermute | solution.py:23
  5.0 9.9 %collective-permute-start.5 = (f32[2,128,128]{2,1,0:T(8,128)S(1)}, f32[2,128,128]{2,1,0:T(8,128)S(1)}, u32[]{:S(2)}, u32[]{:S(2)}) collective-permute-start(f32[2,128,128]{2,1,0:T(8,128)S(1)} %get-tuple-element.68), channel_id=1, source_target_pairs={{1,0},{0,1},{3,2},{2,3},{5,4},{4,5},{7,6},{6,7},{9,8},{8,9},{11,10... | collective-permute-start | bytes 393224 | tf_op jit(solution)/shard_map/ppermute | solution.py:23
  7.0 16.7 %collective-permute-start.2 = (f32[2,128,128]{2,1,0:T(8,128)}, f32[2,128,128]{2,1,0:T(8,128)S(1)}, u32[]{:S(2)}, u32[]{:S(2)}) collective-permute-start(f32[2,128,128]{2,1,0:T(8,128)} %get-tuple-element.69), channel_id=1, source_target_pairs={{1,0},{0,1},{3,2},{2,3},{5,4},{4,5},{7,6},{6,7},{9,8},{8,9},{11,10... | collective-permute-start | bytes 393224 | tf_op jit(solution)/shard_map/ppermute | solution.py:23
  7.8 13.1 %collective-permute-start.4 = (f32[2,128,256]{2,1,0:T(8,128)}, f32[2,128,256]{2,1,0:T(8,128)S(1)}, u32[]{:S(2)}, u32[]{:S(2)}) collective-permute-start(f32[2,128,256]{2,1,0:T(8,128)} %slice.35), channel_id=1, source_target_pairs={{2,0},{4,2},{6,4},{8,6},{10,8},{12,10},{14,12},{16,14},{18,16},{20... | collective-permute-start | bytes 786440 | tf_op jit(solution)/shard_map/ppermute | solution.py:23
  11.2 12.5 %collective-permute-start = (f32[2,128,256]{2,1,0:T(8,128)S(1)}, f32[2,128,256]{2,1,0:T(8,128)S(1)}, u32[]{:S(2)}, u32[]{:S(2)}) collective-permute-start(f32[2,128,256]{2,1,0:T(8,128)S(1)} %slice.32), channel_id=1, source_target_pairs={{2,0},{4,2},{6,4},{8,6},{10,8},{12,10},{14,12},{16,14},{18,16},{20... | collective-permute-start | bytes 786440 | tf_op jit(solution)/shard_map/ppermute | solution.py:23
  13.1 10.6 %collective-permute-start.3 = (f32[2,128,128]{2,1,0:T(8,128)S(1)}, f32[2,128,128]{2,1,0:T(8,128)S(1)}, u32[]{:S(2)}, u32[]{:S(2)}) collective-permute-start(f32[2,128,128]{2,1,0:T(8,128)S(1)} %collective-permute-done.1.upper_ref), channel_id=1, source_target_pairs={{2,0},{4,2},{6,4},{8,6},{10,8},{12,10},{14,12},{16,14},{18,16},{20... | collective-permute-start | bytes 393224 | tf_op jit(solution)/shard_map/ppermute | solution.py:23
  14.9 6.0 %collective-permute-start.7 = (f32[2,128,128]{2,1,0:T(8,128)S(1)}, f32[2,128,128]{2,1,0:T(8,128)S(1)}, u32[]{:S(2)}, u32[]{:S(2)}) collective-permute-start(f32[2,128,128]{2,1,0:T(8,128)S(1)} %collective-permute-done.5.upper_ref), channel_id=1, source_target_pairs={{2,0},{4,2},{6,4},{8,6},{10,8},{12,10},{14,12},{16,14},{18,16},{20... | collective-permute-start | bytes 393224 | tf_op jit(solution)/shard_map/ppermute | solution.py:23
  30.4 7.3 %collective-permute-start.9 = (f32[2,128,128]{2,1,0:T(8,128)S(1)}, f32[2,128,128]{2,1,0:T(8,128)S(1)}, u32[]{:S(2)}, u32[]{:S(2)}) collective-permute-start(f32[2,128,128]{2,1,0:T(8,128)S(1)} %get-tuple-element.39), channel_id=1, source_target_pairs={{30,0},{0,2},{2,4},{4,6},{6,8},{8,10},{10,12},{12,14},{14,16},{16,... | collective-permute-start | bytes 393224 | tf_op jit(solution)/shard_map/ppermute | solution.py:23
  30.5 13.6 %collective-permute-start.8 = (f32[2,128,256]{2,1,0:T(8,128)S(1)}, f32[2,128,256]{2,1,0:T(8,128)S(1)}, u32[]{:S(2)}, u32[]{:S(2)}) collective-permute-start(f32[2,128,256]{2,1,0:T(8,128)S(1)} %get-tuple-element.37), channel_id=1, source_target_pairs={{30,0},{0,2},{2,4},{4,6},{6,8},{8,10},{10,12},{12,14},{14,16},{16,... | collective-permute-start | bytes 786440 | tf_op jit(solution)/shard_map/ppermute | solution.py:23
  30.5 11.4 %collective-permute-start.13 = (f32[2,128,128]{2,1,0:T(8,128)S(1)}, f32[2,128,128]{2,1,0:T(8,128)S(1)}, u32[]{:S(2)}, u32[]{:S(2)}) collective-permute-start(f32[2,128,128]{2,1,0:T(8,128)S(1)} %get-tuple-element.45), channel_id=1, source_target_pairs={{30,0},{0,2},{2,4},{4,6},{6,8},{8,10},{10,12},{12,14},{14,16},{16,... | collective-permute-start | bytes 393224 | tf_op jit(solution)/shard_map/ppermute | solution.py:23
  31.0 12.4 %collective-permute-start.11 = (f32[2,128,128]{2,1,0:T(8,128)S(1)}, f32[2,128,128]{2,1,0:T(8,128)S(1)}, u32[]{:S(2)}, u32[]{:S(2)}) collective-permute-start(f32[2,128,128]{2,1,0:T(8,128)S(1)} %get-tuple-element.40), channel_id=1, source_target_pairs={{1,0},{0,1},{3,2},{2,3},{5,4},{4,5},{7,6},{6,7},{9,8},{8,9},{11,10... | collective-permute-start | bytes 393224 | tf_op jit(solution)/shard_map/ppermute | solution.py:23
  32.5 16.0 %collective-permute-start.12 = (f32[2,128,256]{2,1,0:T(8,128)S(1)}, f32[2,128,256]{2,1,0:T(8,128)S(1)}, u32[]{:S(2)}, u32[]{:S(2)}) collective-permute-start(f32[2,128,256]{2,1,0:T(8,128)S(1)} %get-tuple-element.43), channel_id=1, source_target_pairs={{30,0},{0,2},{2,4},{4,6},{6,8},{8,10},{10,12},{12,14},{14,16},{16,... | collective-permute-start | bytes 786440 | tf_op jit(solution)/shard_map/ppermute | solution.py:23
  37.7 6.3 %collective-permute-start.10 = (f32[2,128,128]{2,1,0:T(8,128)S(1)}, f32[2,128,128]{2,1,0:T(8,128)S(1)}, u32[]{:S(2)}, u32[]{:S(2)}) collective-permute-start(f32[2,128,128]{2,1,0:T(8,128)S(1)} %add.12), channel_id=1, source_target_pairs={{1,0},{0,1},{3,2},{2,3},{5,4},{4,5},{7,6},{6,7},{9,8},{8,9},{11,10... | collective-permute-start | bytes 393224 | tf_op jit(solution)/shard_map/ppermute | solution.py:23
  41.9 5.0 %collective-permute-start.15 = (f32[2,128,128]{2,1,0:T(8,128)S(1)}, f32[2,128,128]{2,1,0:T(8,128)S(1)}, u32[]{:S(2)}, u32[]{:S(2)}) collective-permute-start(f32[2,128,128]{2,1,0:T(8,128)S(1)} %get-tuple-element.46), channel_id=1, source_target_pairs={{1,0},{0,1},{3,2},{2,3},{5,4},{4,5},{7,6},{6,7},{9,8},{8,9},{11,10... | collective-permute-start | bytes 393224 | tf_op jit(solution)/shard_map/ppermute | solution.py:23
  43.4 5.0 %collective-permute-start.14 = (f32[2,128,128]{2,1,0:T(8,128)S(1)}, f32[2,128,128]{2,1,0:T(8,128)S(1)}, u32[]{:S(2)}, u32[]{:S(2)}) collective-permute-start(f32[2,128,128]{2,1,0:T(8,128)S(1)} %add.13), channel_id=1, source_target_pairs={{1,0},{0,1},{3,2},{2,3},{5,4},{4,5},{7,6},{6,7},{9,8},{8,9},{11,10... | collective-permute-start | bytes 393224 | tf_op jit(solution)/shard_map/ppermute | solution.py:23
  44.2 6.6 %collective-permute-start.21 = (f32[2,128,128]{2,1,0:T(8,128)S(1)}, f32[2,128,128]{2,1,0:T(8,128)S(1)}, u32[]{:S(2)}, u32[]{:S(2)}) collective-permute-start(f32[2,128,128]{2,1,0:T(8,128)S(1)} %get-tuple-element.52), channel_id=1, source_target_pairs={{1,0},{0,1},{3,2},{2,3},{5,4},{4,5},{7,6},{6,7},{9,8},{8,9},{11,10... | collective-permute-start | bytes 393224 | tf_op jit(solution)/shard_map/ppermute | solution.py:23
  45.7 13.3 %collective-permute-start.20 = (f32[2,128,256]{2,1,0:T(8,128)S(1)}, f32[2,128,256]{2,1,0:T(8,128)S(1)}, u32[]{:S(2)}, u32[]{:S(2)}) collective-permute-start(f32[2,128,256]{2,1,0:T(8,128)S(1)} %get-tuple-element.51), channel_id=1, source_target_pairs={{2,0},{4,2},{6,4},{8,6},{10,8},{12,10},{14,12},{16,14},{18,16},{20... | collective-permute-start | bytes 786440 | tf_op jit(solution)/shard_map/ppermute | solution.py:23
  48.6 5.5 %collective-permute-start.17 = (f32[2,128,128]{2,1,0:T(8,128)S(1)}, f32[2,128,128]{2,1,0:T(8,128)S(1)}, u32[]{:S(2)}, u32[]{:S(2)}) collective-permute-start(f32[2,128,128]{2,1,0:T(8,128)S(1)} %get-tuple-element.49), channel_id=1, source_target_pairs={{1,0},{0,1},{3,2},{2,3},{5,4},{4,5},{7,6},{6,7},{9,8},{8,9},{11,10... | collective-permute-start | bytes 393224 | tf_op jit(solution)/shard_map/ppermute | solution.py:23
  50.2 11.6 %collective-permute-start.16 = (f32[2,128,256]{2,1,0:T(8,128)S(1)}, f32[2,128,256]{2,1,0:T(8,128)S(1)}, u32[]{:S(2)}, u32[]{:S(2)}) collective-permute-start(f32[2,128,256]{2,1,0:T(8,128)S(1)} %get-tuple-element.48), channel_id=1, source_target_pairs={{2,0},{4,2},{6,4},{8,6},{10,8},{12,10},{14,12},{16,14},{18,16},{20... | collective-permute-start | bytes 786440 | tf_op jit(solution)/shard_map/ppermute | solution.py:23
  50.2 6.7 %collective-permute-start.22 = (f32[2,128,128]{2,1,0:T(8,128)S(1)}, f32[2,128,128]{2,1,0:T(8,128)S(1)}, u32[]{:S(2)}, u32[]{:S(2)}) collective-permute-start(f32[2,128,128]{2,1,0:T(8,128)S(1)} %get-tuple-element.53), channel_id=1, source_target_pairs={{1,0},{0,1},{3,2},{2,3},{5,4},{4,5},{7,6},{6,7},{9,8},{8,9},{11,10... | collective-permute-start | bytes 393224 | tf_op jit(solution)/shard_map/ppermute | solution.py:23
  50.8 8.3 %collective-permute-start.23 = (f32[2,128,128]{2,1,0:T(8,128)S(1)}, f32[2,128,128]{2,1,0:T(8,128)S(1)}, u32[]{:S(2)}, u32[]{:S(2)}) collective-permute-start(f32[2,128,128]{2,1,0:T(8,128)S(1)} %collective-permute-done.21.upper_ref), channel_id=1, source_target_pairs={{2,0},{4,2},{6,4},{8,6},{10,8},{12,10},{14,12},{16,14},{18,16},{20... | collective-permute-start | bytes 393224 | tf_op jit(solution)/shard_map/ppermute | solution.py:23
  54.1 7.8 %collective-permute-start.18 = (f32[2,128,128]{2,1,0:T(8,128)S(1)}, f32[2,128,128]{2,1,0:T(8,128)S(1)}, u32[]{:S(2)}, u32[]{:S(2)}) collective-permute-start(f32[2,128,128]{2,1,0:T(8,128)S(1)} %get-tuple-element.50), channel_id=1, source_target_pairs={{1,0},{0,1},{3,2},{2,3},{5,4},{4,5},{7,6},{6,7},{9,8},{8,9},{11,10... | collective-permute-start | bytes 393224 | tf_op jit(solution)/shard_map/ppermute | solution.py:23
  56.9 5.0 %collective-permute-start.19 = (f32[2,128,128]{2,1,0:T(8,128)S(1)}, f32[2,128,128]{2,1,0:T(8,128)S(1)}, u32[]{:S(2)}, u32[]{:S(2)}) collective-permute-start(f32[2,128,128]{2,1,0:T(8,128)S(1)} %collective-permute-done.17.upper_ref), channel_id=1, source_target_pairs={{2,0},{4,2},{6,4},{8,6},{10,8},{12,10},{14,12},{16,14},{18,16},{20... | collective-permute-start | bytes 393224 | tf_op jit(solution)/shard_map/ppermute | solution.py:23
  65.0 7.3 %collective-permute-start.29 = (f32[2,128,128]{2,1,0:T(8,128)S(1)}, f32[2,128,128]{2,1,0:T(8,128)S(1)}, u32[]{:S(2)}, u32[]{:S(2)}) collective-permute-start(f32[2,128,128]{2,1,0:T(8,128)S(1)} %get-tuple-element.63), channel_id=1, source_target_pairs={{30,0},{0,2},{2,4},{4,6},{6,8},{8,10},{10,12},{12,14},{14,16},{16,... | collective-permute-start | bytes 393224 | tf_op jit(solution)/shard_map/ppermute | solution.py:23
  68.1 7.1 %collective-permute-start.25 = (f32[2,128,128]{2,1,0:T(8,128)S(1)}, f32[2,128,128]{2,1,0:T(8,128)S(1)}, u32[]{:S(2)}, u32[]{:S(2)}) collective-permute-start(f32[2,128,128]{2,1,0:T(8,128)S(1)} %get-tuple-element.58), channel_id=1, source_target_pairs={{30,0},{0,2},{2,4},{4,6},{6,8},{8,10},{10,12},{12,14},{14,16},{16,... | collective-permute-start | bytes 393224 | tf_op jit(solution)/shard_map/ppermute | solution.py:23
  68.2 7.9 %collective-permute-start.31 = (f32[2,128,128]{2,1,0:T(8,128)S(1)}, f32[2,128,128]{2,1,0:T(8,128)S(1)}, u32[]{:S(2)}, u32[]{:S(2)}) collective-permute-start(f32[2,128,128]{2,1,0:T(8,128)S(1)} %get-tuple-element.64), channel_id=1, source_target_pairs={{1,0},{0,1},{3,2},{2,3},{5,4},{4,5},{7,6},{6,7},{9,8},{8,9},{11,10... | collective-permute-start | bytes 393224 | tf_op jit(solution)/shard_map/ppermute | solution.py:23
  69.1 11.2 %collective-permute-start.28 = (f32[2,128,256]{2,1,0:T(8,128)S(1)}, f32[2,128,256]{2,1,0:T(8,128)S(1)}, u32[]{:S(2)}, u32[]{:S(2)}) collective-permute-start(f32[2,128,256]{2,1,0:T(8,128)S(1)} %get-tuple-element.61), channel_id=1, source_target_pairs={{30,0},{0,2},{2,4},{4,6},{6,8},{8,10},{10,12},{12,14},{14,16},{16,... | collective-permute-start | bytes 786440 | tf_op jit(solution)/shard_map/ppermute | solution.py:23
  69.3 12.4 %collective-permute-start.24 = (f32[2,128,256]{2,1,0:T(8,128)S(1)}, f32[2,128,256]{2,1,0:T(8,128)S(1)}, u32[]{:S(2)}, u32[]{:S(2)}) collective-permute-start(f32[2,128,256]{2,1,0:T(8,128)S(1)} %get-tuple-element.56), channel_id=1, source_target_pairs={{30,0},{0,2},{2,4},{4,6},{6,8},{8,10},{10,12},{12,14},{14,16},{16,... | collective-permute-start | bytes 786440 | tf_op jit(solution)/shard_map/ppermute | solution.py:23
  72.3 6.4 %collective-permute-start.27 = (f32[2,128,128]{2,1,0:T(8,128)S(1)}, f32[2,128,128]{2,1,0:T(8,128)S(1)}, u32[]{:S(2)}, u32[]{:S(2)}) collective-permute-start(f32[2,128,128]{2,1,0:T(8,128)S(1)} %get-tuple-element.59), channel_id=1, source_target_pairs={{1,0},{0,1},{3,2},{2,3},{5,4},{4,5},{7,6},{6,7},{9,8},{8,9},{11,10... | collective-permute-start | bytes 393224 | tf_op jit(solution)/shard_map/ppermute | solution.py:23
  75.3 5.0 %collective-permute-start.30 = (f32[2,128,128]{2,1,0:T(8,128)S(1)}, f32[2,128,128]{2,1,0:T(8,128)S(1)}, u32[]{:S(2)}, u32[]{:S(2)}) collective-permute-start(f32[2,128,128]{2,1,0:T(8,128)S(1)} %add.15), channel_id=1, source_target_pairs={{1,0},{0,1},{3,2},{2,3},{5,4},{4,5},{7,6},{6,7},{9,8},{8,9},{11,10... | collective-permute-start | bytes 393224 | tf_op jit(solution)/shard_map/ppermute | solution.py:23
  76.1 5.6 %collective-permute-start.26 = (f32[2,128,128]{2,1,0:T(8,128)S(1)}, f32[2,128,128]{2,1,0:T(8,128)S(1)}, u32[]{:S(2)}, u32[]{:S(2)}) collective-permute-start(f32[2,128,128]{2,1,0:T(8,128)S(1)} %add.14), channel_id=1, source_target_pairs={{1,0},{0,1},{3,2},{2,3},{5,4},{4,5},{7,6},{6,7},{9,8},{8,9},{11,10... | collective-permute-start | bytes 393224 | tf_op jit(solution)/shard_map/ppermute | solution.py:23
  (9 other events, 63.9 us)
where the time goes:
time: 83 us; the launch traced here: 82.9 us
  starting transfers between devices  36 us (43%)
  waiting for transfers between devices  23.1 us (28%)
  Pallas kernels  18.9 us (23%)
  local copies, waits for them, and re-layouts  3.79 us (5%)
  between operations  0.95 us (1%)
    ppermute x32, starting transfers between devices, from_behind(): return lax.ppermute(block, axis, route)  36 us
    ppermute x32, waiting for transfers between devices, from_behind(): return lax.ppermute(block, axis, route)  23.1 us
    pallas_call x9, Pallas kernels, call(): pl.pallas_call(functools.partial(kernel, **static), in_specs=[SMEM] * len...  18.9 us
  transfers between devices with their start and end apart: 32, of which 14 were waited for; matrix products, arithmetic and copies ran while one was open for 2% of the time, Pallas kernels for 10%

commit v1 on v0

--- a/solution.py
+++ b/solution.py
@@ -84,6 +84,10 @@
     ]
 
 
+def slice_of(ref, part):
+    return ref.at[part] if len(ref.shape) == 4 else ref
+
+
 def fill_ext(ext_ref, tile_ref, below_ref, upper_ref, lower_ref, corner_ref, width):
     tile_px = tile_ref.shape[1]
     blocks = tile_px // LANES
@@ -97,9 +101,9 @@
         ext_ref[c, blocks, tile_px:, :] = corner_ref[c]
 
 
-def place(pos_ref, j):
-    col = pos_ref[2 * j + 1]
-    return pos_ref[2 * j], col // LANES, col % LANES
+def place(scalar_ref, j):
+    col = scalar_ref[2 * j + 1]
+    return scalar_ref[2 * j], col // LANES, col % LANES
 
 
 def window(ext_ref, c, spot, width, lane):
@@ -135,14 +139,14 @@
 
 
 def forward_kernel(
-    pos_ref, tile_ref, below_ref, upper_ref, lower_ref, corner_ref, probe_ref, prop_ref,
-    rh_ref, rl_ref, lh_ref, ll_ref, moved_ref, ext_ref, a_ref, b_ref, *, spots, width,
+    scalar_ref, tile_ref, below_ref, upper_ref, lower_ref, corner_ref, probe_ref, prop_ref,
+    rh_ref, rl_ref, lh_ref, ll_ref, moved_ref, ext_ref, a_ref, b_ref, *, spots, width, part,
 ):
     tables = (rh_ref, rl_ref, lh_ref, ll_ref)
-    fill_ext(ext_ref, tile_ref, below_ref, upper_ref, lower_ref, corner_ref, width)
+    fill_ext(ext_ref, slice_of(tile_ref, part), below_ref, upper_ref, lower_ref, corner_ref, width)
     lane = lanes_of(width)
     for j in range(spots):
-        spot = place(pos_ref, j)
+        spot = place(scalar_ref, j)
         real = window(ext_ref, 0, spot, width, lane)
         imag = window(ext_ref, 1, spot, width, lane)
         put(
@@ -162,16 +166,16 @@
 
 
 def middle_kernel(
-    pos_ref, count_ref, slot_ref, tile_ref, below_ref, upper_ref, lower_ref, corner_ref,
+    scalar_ref, tile_ref, below_ref, upper_ref, lower_ref, corner_ref,
     moved_ref, amp_ref, rh_ref, rl_ref, lh_ref, ll_ref,
     own_ref, down_ref, up_out_ref, low_out_ref, diag_ref, back_ref,
-    ext_ref, win_ref, a_ref, b_ref, *, spots, width,
+    ext_ref, win_ref, a_ref, b_ref, *, spots, width, part,
 ):
     tables = (rh_ref, rl_ref, lh_ref, ll_ref)
-    fill_ext(ext_ref, tile_ref, below_ref, upper_ref, lower_ref, corner_ref, width)
+    fill_ext(ext_ref, slice_of(tile_ref, part), below_ref, upper_ref, lower_ref, corner_ref, width)
     lane = lanes_of(width)
-    total = count_ref[0]
-    spot_list = [place(pos_ref, j) for j in range(spots)]
+    total = scalar_ref[2 * spots]
+    spot_list = [place(scalar_ref, j) for j in range(spots)]
     for j in range(spots):
         second_real = window(ext_ref, 0, spot_list[j], width, lane)
         second_imag = window(ext_ref, 1, spot_list[j], width, lane)
@@ -184,7 +188,7 @@
         )
     ext_ref[...] = jnp.zeros(ext_ref.shape, jnp.float32)
     for j, (real, imag) in enumerate(transform(a_ref, b_ref, tables, spots, width)):
-        measured = amp_ref[slot_ref[j]]
+        measured = amp_ref[scalar_ref[2 * spots + 1 + j]]
         power = jnp.maximum(real * real + imag * imag, floor_amp * floor_amp)
         factor = 1.0 - measured * lax.rsqrt(power)
         put(a_ref, j, width, real * factor, -(imag * factor))
@@ -199,13 +203,13 @@
 
 
 def backward_kernel(
-    pos_ref, count_ref, back_ref, probe_ref, prop_ref, rh_ref, rl_ref, lh_ref, ll_ref,
+    scalar_ref, back_ref, probe_ref, prop_ref, rh_ref, rl_ref, lh_ref, ll_ref,
     own_ref, down_ref, up_out_ref, low_out_ref, diag_ref,
     ext_ref, a_ref, b_ref, *, spots, width,
 ):
     tables = (rh_ref, rl_ref, lh_ref, ll_ref)
     lane = lanes_of(width)
-    total = count_ref[0]
+    total = scalar_ref[2 * spots]
     for j in range(spots):
         put(a_ref, j, width, back_ref[j, 0], back_ref[j, 1])
     ext_ref[...] = jnp.zeros(ext_ref.shape, jnp.float32)
@@ -217,7 +221,7 @@
         )
     for j, (real, negative) in enumerate(transform(a_ref, b_ref, tables, spots, width)):
         imag = -negative
-        spot = place(pos_ref, j)
+        spot = place(scalar_ref, j)
         used = j < total
         scatter(ext_ref, 0, spot, width, lane, used, probe_ref[0] * real + probe_ref[1] * imag)
         scatter(ext_ref, 1, spot, width, lane, used, probe_ref[0] * imag - probe_ref[1] * real)
@@ -238,8 +242,9 @@
 
 def update_kernel(
     tile_ref, own_ref, above_ref, upper_ref, lower_ref,
-    new_ref, top_ref, left_up_ref, left_low_ref, *, width,
+    new_ref, top_ref, left_up_ref, left_low_ref, *, width, part,
 ):
+    tile_ref = slice_of(tile_ref, part)
     for c in range(2):
         for k, (rows, lanes, value) in enumerate(
             folded(tile_ref, own_ref, above_ref, upper_ref, lower_ref, c, width)
@@ -267,7 +272,7 @@
 LIMIT = pltpu.CompilerParams(vmem_limit_bytes=16 * 1024 * 1024)
 
 
-def call(kernel, scalars, arrays, outs, scratch, name, **static):
+def call(kernel, scalars, arrays, outs, scratch, **static):
     return pl.pallas_call(
         functools.partial(kernel, **static),
         in_specs=[SMEM] * len(scalars) + [VMEM] * len(arrays),
@@ -275,8 +280,24 @@
         out_shape=outs,
         scratch_shapes=scratch,
         compiler_params=LIMIT,
-        name=name,
     )(*scalars, *arrays)
+
+
+def pack_kernel(whole_ref, *refs, width):
+    outs, sems = refs[:-1], refs[-1]
+    tile_px = whole_ref.shape[2]
+    copies = []
+    for s in range(2):
+        up, low, top = outs[3 * s:3 * s + 3]
+        left = pl.ds(0, width)
+        copies.append((whole_ref.at[s, :, pl.ds(0, width), left], up))
+        copies.append((whole_ref.at[s, :, pl.ds(width, tile_px - width), left], low))
+        copies.append((whole_ref.at[s, :, pl.ds(0, width), :], top))
+    copies = [pltpu.make_async_copy(a, b, sems.at[k]) for k, (a, b) in enumerate(copies)]
+    for copy in copies:
+        copy.start()
+    for copy in copies:
+        copy.wait()
 
 
 def body(
@@ -294,9 +315,7 @@
     ext = tile_px + width
     tables = [jnp.asarray(t) for t in dft_operands(width)]
     prop = jnp.stack([jnp.cos(propagation_phase), jnp.sin(propagation_phase)])
-    where = positions.reshape(-1)
-    count = counts.reshape(-1)
-    slots = measurement_index.reshape(-1)
+    scalars = (jnp.concatenate([positions.reshape(-1), counts.reshape(-1), measurement_index.reshape(-1)]),)
     measured = amplitudes[0, 0]
     static = dict(spots=spots, width=width)
     ext_space = pltpu.VMEM((2, ext // LANES, ext, LANES), jnp.float32)
@@ -310,7 +329,7 @@
     strip = F32((2, width, tile_px))
     gradient = [whole, strip, square, square, square]
 
-    def halo(top, left_up, left_low):
+    def halo(left_up, left_low, top):
         upper = from_behind(left_up, "col", -1)
         lower = from_behind(left_low, "col", -1)
         below = from_behind(top, "row", -1)
@@ -324,40 +343,49 @@
         upper = from_behind(side_up + corner, "col", 1)
         return own, above, upper, lower
 
-    tiles = [specimen_slices[0], specimen_slices[1]]
-    sends = [(t[:, :width, :], t[:, :width, :width], t[:, width:, :width]) for t in tiles]
-    for iteration in range(ITERS):
+    packed = pl.pallas_call(
+        functools.partial(pack_kernel, width=width),
+        in_specs=[pl.BlockSpec(memory_space=pl.ANY)],
+        out_specs=[VMEM] * 6,
+        out_shape=[square, square, strip] * 2,
+        scratch_shapes=[pltpu.SemaphoreType.DMA((6,))],
+        compiler_params=LIMIT,
+        name="pack",
+    )(specimen_slices)
+    tiles = [specimen_slices, specimen_slices]
+    sends = [packed[:3], packed[3:]]
+    for i in range(ITERS):
         halo_one = halo(*sends[0])
         halo_two = halo(*sends[1])
         (moved,) = call(
-            forward_kernel, (where,), (tiles[0], *halo_one, illumination_probe, prop, *tables),
-            [wave], [ext_space, *work], "forward_wave", **static,
+            forward_kernel, scalars, (tiles[0], *halo_one, illumination_probe, prop, *tables),
+            [wave], [ext_space, *work], part=0, **static,
         )
         *grad_two, back = call(
-            middle_kernel, (where, count, slots), (tiles[1], *halo_two, moved, measured, *tables),
+            middle_kernel, scalars, (tiles[1], *halo_two, moved, measured, *tables),
             [*gradient, wave], [ext_space, pltpu.VMEM((spots, 2, width, width), jnp.float32), *work],
-            "residual_wave", **static,
+            part=1, **static,
         )
         fold_two = fold(*grad_two)
         grad_one = call(
-            backward_kernel, (where, count), (back, illumination_probe, prop, *tables),
-            gradient, [ext_space, *work], "backward_wave", **static,
+            backward_kernel, scalars, (back, illumination_probe, prop, *tables),
+            gradient, [ext_space, *work], **static,
         )
         fold_one = fold(*grad_one)
-        if iteration + 1 < ITERS:
+        if i + 1 < ITERS:
             fresh, sends = [], []
-            for tile, received in zip(tiles, (fold_one, fold_two)):
-                new, *send = call(
+            for part, (tile, received) in enumerate(zip(tiles, (fold_one, fold_two))):
+                new, top, left_up, left_low = call(
                     update_kernel, (), (tile, *received), [whole, strip, square, square], [],
-                    "update_slice", width=width,
+                    width=width, part=part,
                 )
                 fresh.append(new)
-                sends.append(send)
+                sends.append((left_up, left_low, top))
             tiles = fresh
         else:
             (updated,) = call(
                 finish_kernel, (), (tiles[0], *fold_one, tiles[1], *fold_two),
-                [F32(specimen_slices.shape)], [], "finish", width=width,
+                [F32(specimen_slices.shape)], [], width=width,
             )
     return updated
 
@@ -372,6 +400,7 @@
         P("row", "col"),
         P("row", "col", None),
     )
+
     return jax.shard_map(
         body, mesh=mesh, in_specs=placed, out_specs=P(None, None, "row", "col"), check_vma=False
     )

time: 83 us -> 84.7 us (1.020)
  local copies, waits for them, and re-layouts: 3.79 us -> 5.27 us
  waiting for transfers between devices: 23.1 us -> 22.1 us
    unnamed x19 -> x25, local copies, waits for them, and re-layouts: 0.77 us -> 4.11 us
    slice x4 -> x0, local copies, waits for them, and re-layouts: 1.42 us -> none  [the longest x2 0.74 us: body(): t[:, :width, :]]
    squeeze x1 -> x0, local copies, waits for them, and re-layouts: 1.27 us -> none  [body(): tiles = [specimen_slices[0], specimen_slices[1]]]
    ppermute x32, waiting for transfers between devices: 23.1 us -> 22.1 us  [from_behind(): return lax.ppermute(block, axis, route)]
  transfers between devices with their start and end apart: 32 -> 32, of which waited for: 14 -> 13; matrix products, arithmetic and copies ran while one was open for 2% -> 2% of each run, Pallas kernels for 10% -> 10%
where the time goes in v1:
time: 84.7 us; the launch traced here: 84.4 us
  starting transfers between devices  36.8 us (43%)
  waiting for transfers between devices  22.1 us (26%)
  Pallas kernels  19.1 us (23%)
  local copies, waits for them, and re-layouts  5.27 us (6%)
  between operations  0.93 us (1%)
    ppermute x32, starting transfers between devices, from_behind(): return lax.ppermute(block, axis, route)  36.8 us
    ppermute x32, waiting for transfers between devices, from_behind(): return lax.ppermute(block, axis, route)  22.1 us
    pallas_call x9, Pallas kernels, call(): pl.pallas_call(functools.partial(kernel, **static), in_specs=[SMEM] * len...  19 us
    unnamed x25, local copies, waits for them, and re-layouts  4.11 us
  transfers between devices with their start and end apart: 32, of which 13 were waited for; matrix products, arithmetic and copies ran while one was open for 2% of the time, Pallas kernels for 10%

profile of v1, /device:TPU:0, one launch (start us, length us, event | category | flops | bytes accessed | tf_op | source)
XLA Modules:
  0.0 84.4 jit_solution(14343162565166466442)
XLA Ops:
  0.0 1.2 %copy-done = f32[2,2,256,256]{3,2,1,0:T(8,128)S(1)} copy-done((f32[2,2,256,256]{3,2,1,0:T(8,128)S(1)}, f32[2,2,256,256]{3,2,1,0:T(8,128)}, u32[]{:S(2)}) %copy-start) | copy-done | bytes 1048600
  1.4 3.0 %collective-permute-start.1 = (f32[2,128,128]{2,1,0:T(8,128)S(1)}, f32[2,128,128]{2,1,0:T(8,128)S(1)}, u32[]{:S(2)}, u32[]{:S(2)}) collective-permute-start(f32[2,128,128]{2,1,0:T(8,128)S(1)} %get-tuple-element.42), channel_id=1, source_target_pairs={{1,0},{0,1},{3,2},{2,3},{5,4},{4,5},{7,6},{6,7},{9,8},{8,9},{11,10... | collective-permute-start | bytes 393224 | tf_op jit(solution)/shard_map/ppermute | solution.py:23
  4.5 1.9 %collective-permute-start.6 = (f32[2,128,128]{2,1,0:T(8,128)S(1)}, f32[2,128,128]{2,1,0:T(8,128)S(1)}, u32[]{:S(2)}, u32[]{:S(2)}) collective-permute-start(f32[2,128,128]{2,1,0:T(8,128)S(1)} %get-tuple-element.46), channel_id=1, source_target_pairs={{1,0},{0,1},{3,2},{2,3},{5,4},{4,5},{7,6},{6,7},{9,8},{8,9},{11,10... | collective-permute-start | bytes 393224 | tf_op jit(solution)/shard_map/ppermute | solution.py:23
  6.4 3.2 %collective-permute-start = (f32[2,128,256]{2,1,0:T(8,128)S(1)}, f32[2,128,256]{2,1,0:T(8,128)S(1)}, u32[]{:S(2)}, u32[]{:S(2)}) collective-permute-start(f32[2,128,256]{2,1,0:T(8,128)S(1)} %get-tuple-element.41), channel_id=1, source_target_pairs={{2,0},{4,2},{6,4},{8,6},{10,8},{12,10},{14,12},{16,14},{18,16},{20... | collective-permute-start | bytes 786440 | tf_op jit(solution)/shard_map/ppermute | solution.py:23
  9.6 1.5 %collective-permute-start.4 = (f32[2,128,256]{2,1,0:T(8,128)S(1)}, f32[2,128,256]{2,1,0:T(8,128)S(1)}, u32[]{:S(2)}, u32[]{:S(2)}) collective-permute-start(f32[2,128,256]{2,1,0:T(8,128)S(1)} %get-tuple-element.44), channel_id=1, source_target_pairs={{2,0},{4,2},{6,4},{8,6},{10,8},{12,10},{14,12},{16,14},{18,16},{20... | collective-permute-start | bytes 786440 | tf_op jit(solution)/shard_map/ppermute | solution.py:23
  14.1 2.8 %collective-permute-start.7 = (f32[2,128,128]{2,1,0:T(8,128)S(1)}, f32[2,128,128]{2,1,0:T(8,128)S(1)}, u32[]{:S(2)}, u32[]{:S(2)}) collective-permute-start(f32[2,128,128]{2,1,0:T(8,128)S(1)} %collective-permute-done.5.upper_ref), channel_id=1, source_target_pairs={{2,0},{4,2},{6,4},{8,6},{10,8},{12,10},{14,12},{16,14},{18,16},{20... | collective-permute-start | bytes 393224 | tf_op jit(solution)/shard_map/ppermute | solution.py:23
  17.0 2.4 %collective-permute-done.7.corner_ref = f32[2,128,128]{2,1,0:T(8,128)S(1)} collective-permute-done((f32[2,128,128]{2,1,0:T(8,128)S(1)}, f32[2,128,128]{2,1,0:T(8,128)S(1)}, u32[]{:S(2)}, u32[]{:S(2)}) %collective-permute-start.7) | collective-permute-done | bytes 131104 | tf_op jit(solution)/shard_map/ppermute | solution.py:23
  22.2 2.8 %shard_map.109.moved_ref = f32[4,2,128,128]{3,2,1,0:T(8,128)S(1)} custom-call(s32[13]{0:T(128)S(1)} %pad_add_fusion.scalar_ref, f32[2,2,256,256]{3,2,1,0:T(8,128)S(1)} %copy-done.1, f32[2,128,256]{2,1,0:T(8,128)S(1)} %collective-permute-done.4.below_ref, f32[2,128,128]{2,1,0:T(8,128)S(1)} %collective-permute-done.5.upper_ref, ...), custom_call_target="tpu_custom_call" | custom-call | tf_op jit(solution)/shard_map/pallas_call | solution.py:276
  25.1 3.1 %shard_map.110 = (f32[2,256,256]{2,1,0:T(8,128)S(1)}, f32[2,128,256]{2,1,0:T(8,128)S(1)}, f32[2,128,128]{2,1,0:T(8,128)S(1)}, f32[2,128,128]{2,1,0:T(8,128)S(1)}...) custom-call(s32[13]{0:T(128)S(1)} %pad_add_fusion.scalar_ref, f32[2,2,256,256]{3,2,1,0:T(8,128)S(1)} %copy-done.1, ...), custom_call_target="tpu_custom_call" | custom-call | tf_op jit(solution)/shard_map/pallas_call | solution.py:276
  28.2 2.9 %shard_map.111 = (f32[2,256,256]{2,1,0:T(8,128)S(1)}, f32[2,128,256]{2,1,0:T(8,128)S(1)}, f32[2,128,128]{2,1,0:T(8,128)S(1)}, f32[2,128,128]{2,1,0:T(8,128)S(1)}, f32[2,128,128]{2,1,0:T(8,128)S(1)}) custom-call(s32[13]{0:T(128)S(1)} %pad_add_fusion.scalar_ref, f32[4,2,128,128]{3,2,1,0:T(8,128)S(1)} %get-tuple-element.47.back_ref, ...), custom_call_target="tpu_custom_call" | custom-call | tf_op jit(solution)/shard_map/pallas_call | solution.py:276
  31.2 1.3 %collective-permute-start.13 = (f32[2,128,128]{2,1,0:T(8,128)S(1)}, f32[2,128,128]{2,1,0:T(8,128)S(1)}, u32[]{:S(2)}, u32[]{:S(2)}) collective-permute-start(f32[2,128,128]{2,1,0:T(8,128)S(1)} %get-tuple-element.57), channel_id=1, source_target_pairs={{30,0},{0,2},{2,4},{4,6},{6,8},{8,10},{10,12},{12,14},{14,16},{16,... | collective-permute-start | bytes 393224 | tf_op jit(solution)/shard_map/ppermute | solution.py:23
  32.6 1.5 %collective-permute-start.11 = (f32[2,128,128]{2,1,0:T(8,128)S(1)}, f32[2,128,128]{2,1,0:T(8,128)S(1)}, u32[]{:S(2)}, u32[]{:S(2)}) collective-permute-start(f32[2,128,128]{2,1,0:T(8,128)S(1)} %get-tuple-element.52), channel_id=1, source_target_pairs={{1,0},{0,1},{3,2},{2,3},{5,4},{4,5},{7,6},{6,7},{9,8},{8,9},{11,10... | collective-permute-start | bytes 393224 | tf_op jit(solution)/shard_map/ppermute | solution.py:23
  34.1 4.3 %collective-permute-done.9 = f32[2,128,128]{2,1,0:T(8,128)S(1)} collective-permute-done((f32[2,128,128]{2,1,0:T(8,128)S(1)}, f32[2,128,128]{2,1,0:T(8,128)S(1)}, u32[]{:S(2)}, u32[]{:S(2)}) %collective-permute-start.9) | collective-permute-done | bytes 131104 | tf_op jit(solution)/shard_map/ppermute | solution.py:23
  38.4 1.6 %collective-permute-start.10 = (f32[2,128,128]{2,1,0:T(8,128)S(1)}, f32[2,128,128]{2,1,0:T(8,128)S(1)}, u32[]{:S(2)}, u32[]{:S(2)}) collective-permute-start(f32[2,128,128]{2,1,0:T(8,128)S(1)} %add.12), channel_id=1, source_target_pairs={{1,0},{0,1},{3,2},{2,3},{5,4},{4,5},{7,6},{6,7},{9,8},{8,9},{11,10... | collective-permute-start | bytes 393224 | tf_op jit(solution)/shard_map/ppermute | solution.py:23
  40.0 2.6 %collective-permute-done.13 = f32[2,128,128]{2,1,0:T(8,128)S(1)} collective-permute-done((f32[2,128,128]{2,1,0:T(8,128)S(1)}, f32[2,128,128]{2,1,0:T(8,128)S(1)}, u32[]{:S(2)}, u32[]{:S(2)}) %collective-permute-start.13) | collective-permute-done | bytes 131104 | tf_op jit(solution)/shard_map/ppermute | solution.py:23
  42.6 1.5 %collective-permute-start.15 = (f32[2,128,128]{2,1,0:T(8,128)S(1)}, f32[2,128,128]{2,1,0:T(8,128)S(1)}, u32[]{:S(2)}, u32[]{:S(2)}) collective-permute-start(f32[2,128,128]{2,1,0:T(8,128)S(1)} %get-tuple-element.58), channel_id=1, source_target_pairs={{1,0},{0,1},{3,2},{2,3},{5,4},{4,5},{7,6},{6,7},{9,8},{8,9},{11,10... | collective-permute-start | bytes 393224 | tf_op jit(solution)/shard_map/ppermute | solution.py:23
  45.0 1.6 %collective-permute-start.21 = (f32[2,128,128]{2,1,0:T(8,128)S(1)}, f32[2,128,128]{2,1,0:T(8,128)S(1)}, u32[]{:S(2)}, u32[]{:S(2)}) collective-permute-start(f32[2,128,128]{2,1,0:T(8,128)S(1)} %get-tuple-element.64), channel_id=1, source_target_pairs={{1,0},{0,1},{3,2},{2,3},{5,4},{4,5},{7,6},{6,7},{9,8},{8,9},{11,10... | collective-permute-start | bytes 393224 | tf_op jit(solution)/shard_map/ppermute | solution.py:23
  47.6 1.6 %collective-permute-done.14.upper_ref = f32[2,128,128]{2,1,0:T(8,128)S(1)} collective-permute-done((f32[2,128,128]{2,1,0:T(8,128)S(1)}, f32[2,128,128]{2,1,0:T(8,128)S(1)}, u32[]{:S(2)}, u32[]{:S(2)}) %collective-permute-start.14) | collective-permute-done | bytes 131104 | tf_op jit(solution)/shard_map/ppermute | solution.py:23
  49.3 1.5 %collective-permute-start.17 = (f32[2,128,128]{2,1,0:T(8,128)S(1)}, f32[2,128,128]{2,1,0:T(8,128)S(1)}, u32[]{:S(2)}, u32[]{:S(2)}) collective-permute-start(f32[2,128,128]{2,1,0:T(8,128)S(1)} %get-tuple-element.61), channel_id=1, source_target_pairs={{1,0},{0,1},{3,2},{2,3},{5,4},{4,5},{7,6},{6,7},{9,8},{8,9},{11,10... | collective-permute-start | bytes 393224 | tf_op jit(solution)/shard_map/ppermute | solution.py:23
  51.4 3.1 %collective-permute-start.23 = (f32[2,128,128]{2,1,0:T(8,128)S(1)}, f32[2,128,128]{2,1,0:T(8,128)S(1)}, u32[]{:S(2)}, u32[]{:S(2)}) collective-permute-start(f32[2,128,128]{2,1,0:T(8,128)S(1)} %collective-permute-done.21.upper_ref), channel_id=1, source_target_pairs={{2,0},{4,2},{6,4},{8,6},{10,8},{12,10},{14,12},{16,14},{18,16},{20... | collective-permute-start | bytes 393224 | tf_op jit(solution)/shard_map/ppermute | solution.py:23
  54.7 2.3 %collective-permute-start.18 = (f32[2,128,128]{2,1,0:T(8,128)S(1)}, f32[2,128,128]{2,1,0:T(8,128)S(1)}, u32[]{:S(2)}, u32[]{:S(2)}) collective-permute-start(f32[2,128,128]{2,1,0:T(8,128)S(1)} %get-tuple-element.62), channel_id=1, source_target_pairs={{1,0},{0,1},{3,2},{2,3},{5,4},{4,5},{7,6},{6,7},{9,8},{8,9},{11,10... | collective-permute-start | bytes 393224 | tf_op jit(solution)/shard_map/ppermute | solution.py:23
  57.5 2.2 %collective-permute-start.19 = (f32[2,128,128]{2,1,0:T(8,128)S(1)}, f32[2,128,128]{2,1,0:T(8,128)S(1)}, u32[]{:S(2)}, u32[]{:S(2)}) collective-permute-start(f32[2,128,128]{2,1,0:T(8,128)S(1)} %collective-permute-done.17.upper_ref), channel_id=1, source_target_pairs={{2,0},{4,2},{6,4},{8,6},{10,8},{12,10},{14,12},{16,14},{18,16},{20... | collective-permute-start | bytes 393224 | tf_op jit(solution)/shard_map/ppermute | solution.py:23
  59.8 2.8 %shard_map.114.moved_ref = f32[4,2,128,128]{3,2,1,0:T(8,128)S(1)} custom-call(s32[13]{0:T(128)S(1)} %pad_add_fusion.scalar_ref, f32[2,256,256]{2,1,0:T(8,128)S(1)} %get-tuple-element.53.tile_ref.refs_0_, f32[2,128,256]{2,1,0:T(8,128)S(1)} %collective-permute-done.20.below_ref, f32[2,128,128]{2,1,0:T(8,128)S(1)} %collective-permute-done.21.upper_ref, ...), custom_call_target="tpu_custom_call" | custom-call | tf_op jit(solution)/shard_map/pallas_call | solution.py:276
  62.6 3.1 %shard_map.115 = (f32[2,256,256]{2,1,0:T(8,128)S(1)}, f32[2,128,256]{2,1,0:T(8,128)S(1)}, f32[2,128,128]{2,1,0:T(8,128)S(1)}, f32[2,128,128]{2,1,0:T(8,128)S(1)}...) custom-call(s32[13]{0:T(128)S(1)} %pad_add_fusion.scalar_ref, ...), custom_call_target="tpu_custom_call" | custom-call | tf_op jit(solution)/shard_map/pallas_call | solution.py:276
  66.0 2.9 %shard_map.116 = (f32[2,256,256]{2,1,0:T(8,128)S(1)}, f32[2,128,256]{2,1,0:T(8,128)S(1)}, f32[2,128,128]{2,1,0:T(8,128)S(1)}, f32[2,128,128]{2,1,0:T(8,128)S(1)}, f32[2,128,128]{2,1,0:T(8,128)S(1)}) custom-call(s32[13]{0:T(128)S(1)} %pad_add_fusion.scalar_ref, f32[4,2,128,128]{3,2,1,0:T(8,128)S(1)} %get-tuple-element.66.back_ref, ...), custom_call_target="tpu_custom_call" | custom-call | tf_op jit(solution)/shard_map/pallas_call | solution.py:276
  69.6 1.3 %collective-permute-start.28 = (f32[2,128,256]{2,1,0:T(8,128)S(1)}, f32[2,128,256]{2,1,0:T(8,128)S(1)}, u32[]{:S(2)}, u32[]{:S(2)}) collective-permute-start(f32[2,128,256]{2,1,0:T(8,128)S(1)} %get-tuple-element.73), channel_id=1, source_target_pairs={{30,0},{0,2},{2,4},{4,6},{6,8},{8,10},{10,12},{12,14},{14,16},{16,... | collective-permute-start | bytes 786440 | tf_op jit(solution)/shard_map/ppermute | solution.py:23
  71.3 1.7 %collective-permute-done.29 = f32[2,128,128]{2,1,0:T(8,128)S(1)} collective-permute-done((f32[2,128,128]{2,1,0:T(8,128)S(1)}, f32[2,128,128]{2,1,0:T(8,128)S(1)}, u32[]{:S(2)}, u32[]{:S(2)}) %collective-permute-start.29) | collective-permute-done | bytes 131104 | tf_op jit(solution)/shard_map/ppermute | solution.py:23
  73.6 2.4 %collective-permute-done.25 = f32[2,128,128]{2,1,0:T(8,128)S(1)} collective-permute-done((f32[2,128,128]{2,1,0:T(8,128)S(1)}, f32[2,128,128]{2,1,0:T(8,128)S(1)}, u32[]{:S(2)}, u32[]{:S(2)}) %collective-permute-start.25) | collective-permute-done | bytes 131104 | tf_op jit(solution)/shard_map/ppermute | solution.py:23
  76.6 1.5 %collective-permute-start.26 = (f32[2,128,128]{2,1,0:T(8,128)S(1)}, f32[2,128,128]{2,1,0:T(8,128)S(1)}, u32[]{:S(2)}, u32[]{:S(2)}) collective-permute-start(f32[2,128,128]{2,1,0:T(8,128)S(1)} %add.14), channel_id=1, source_target_pairs={{1,0},{0,1},{3,2},{2,3},{5,4},{4,5},{7,6},{6,7},{9,8},{8,9},{11,10... | collective-permute-start | bytes 393224 | tf_op jit(solution)/shard_map/ppermute | solution.py:23
  78.1 1.3 %collective-permute-done.27.refs_4_ = f32[2,128,128]{2,1,0:T(8,128)S(1)} collective-permute-done((f32[2,128,128]{2,1,0:T(8,128)S(1)}, f32[2,128,128]{2,1,0:T(8,128)S(1)}, u32[]{:S(2)}, u32[]{:S(2)}) %collective-permute-start.27) | collective-permute-done | bytes 131104 | tf_op jit(solution)/shard_map/ppermute | solution.py:23
  79.4 2.4 %collective-permute-done.30.refs_8_ = f32[2,128,128]{2,1,0:T(8,128)S(1)} collective-permute-done((f32[2,128,128]{2,1,0:T(8,128)S(1)}, f32[2,128,128]{2,1,0:T(8,128)S(1)}, u32[]{:S(2)}, u32[]{:S(2)}) %collective-permute-start.30) | collective-permute-done | bytes 131104 | tf_op jit(solution)/shard_map/ppermute | solution.py:23
  81.8 1.4 %collective-permute-done.26.refs_3_ = f32[2,128,128]{2,1,0:T(8,128)S(1)} collective-permute-done((f32[2,128,128]{2,1,0:T(8,128)S(1)}, f32[2,128,128]{2,1,0:T(8,128)S(1)}, u32[]{:S(2)}, u32[]{:S(2)}) %collective-permute-start.26) | collective-permute-done | bytes 131104 | tf_op jit(solution)/shard_map/ppermute | solution.py:23
  (75 shorter events, 12.6 us)
Async XLA Ops:
  1.4 11.7 %collective-permute-start.1 = (f32[2,128,128]{2,1,0:T(8,128)S(1)}, f32[2,128,128]{2,1,0:T(8,128)S(1)}, u32[]{:S(2)}, u32[]{:S(2)}) collective-permute-start(f32[2,128,128]{2,1,0:T(8,128)S(1)} %get-tuple-element.42), channel_id=1, source_target_pairs={{1,0},{0,1},{3,2},{2,3},{5,4},{4,5},{7,6},{6,7},{9,8},{8,9},{11,10... | collective-permute-start | bytes 393224 | tf_op jit(solution)/shard_map/ppermute | solution.py:23
  4.4 9.2 %collective-permute-start.5 = (f32[2,128,128]{2,1,0:T(8,128)S(1)}, f32[2,128,128]{2,1,0:T(8,128)S(1)}, u32[]{:S(2)}, u32[]{:S(2)}) collective-permute-start(f32[2,128,128]{2,1,0:T(8,128)S(1)} %get-tuple-element.45), channel_id=1, source_target_pairs={{1,0},{0,1},{3,2},{2,3},{5,4},{4,5},{7,6},{6,7},{9,8},{8,9},{11,10... | collective-permute-start | bytes 393224 | tf_op jit(solution)/shard_map/ppermute | solution.py:23
  4.5 9.6 %collective-permute-start.6 = (f32[2,128,128]{2,1,0:T(8,128)S(1)}, f32[2,128,128]{2,1,0:T(8,128)S(1)}, u32[]{:S(2)}, u32[]{:S(2)}) collective-permute-start(f32[2,128,128]{2,1,0:T(8,128)S(1)} %get-tuple-element.46), channel_id=1, source_target_pairs={{1,0},{0,1},{3,2},{2,3},{5,4},{4,5},{7,6},{6,7},{9,8},{8,9},{11,10... | collective-permute-start | bytes 393224 | tf_op jit(solution)/shard_map/ppermute | solution.py:23
  6.4 18.6 %collective-permute-start = (f32[2,128,256]{2,1,0:T(8,128)S(1)}, f32[2,128,256]{2,1,0:T(8,128)S(1)}, u32[]{:S(2)}, u32[]{:S(2)}) collective-permute-start(f32[2,128,256]{2,1,0:T(8,128)S(1)} %get-tuple-element.41), channel_id=1, source_target_pairs={{2,0},{4,2},{6,4},{8,6},{10,8},{12,10},{14,12},{16,14},{18,16},{20... | collective-permute-start | bytes 786440 | tf_op jit(solution)/shard_map/ppermute | solution.py:23
  9.6 9.8 %collective-permute-start.4 = (f32[2,128,256]{2,1,0:T(8,128)S(1)}, f32[2,128,256]{2,1,0:T(8,128)S(1)}, u32[]{:S(2)}, u32[]{:S(2)}) collective-permute-start(f32[2,128,256]{2,1,0:T(8,128)S(1)} %get-tuple-element.44), channel_id=1, source_target_pairs={{2,0},{4,2},{6,4},{8,6},{10,8},{12,10},{14,12},{16,14},{18,16},{20... | collective-permute-start | bytes 786440 | tf_op jit(solution)/shard_map/ppermute | solution.py:23
  13.0 11.9 %collective-permute-start.2 = (f32[2,128,128]{2,1,0:T(8,128)S(1)}, f32[2,128,128]{2,1,0:T(8,128)S(1)}, u32[]{:S(2)}, u32[]{:S(2)}) collective-permute-start(f32[2,128,128]{2,1,0:T(8,128)S(1)} %get-tuple-element.43), channel_id=1, source_target_pairs={{1,0},{0,1},{3,2},{2,3},{5,4},{4,5},{7,6},{6,7},{9,8},{8,9},{11,10... | collective-permute-start | bytes 393224 | tf_op jit(solution)/shard_map/ppermute | solution.py:23
  13.6 11.4 %collective-permute-start.3 = (f32[2,128,128]{2,1,0:T(8,128)S(1)}, f32[2,128,128]{2,1,0:T(8,128)S(1)}, u32[]{:S(2)}, u32[]{:S(2)}) collective-permute-start(f32[2,128,128]{2,1,0:T(8,128)S(1)} %collective-permute-done.1.upper_ref), channel_id=1, source_target_pairs={{2,0},{4,2},{6,4},{8,6},{10,8},{12,10},{14,12},{16,14},{18,16},{20... | collective-permute-start | bytes 393224 | tf_op jit(solution)/shard_map/ppermute | solution.py:23
  14.1 5.3 %collective-permute-start.7 = (f32[2,128,128]{2,1,0:T(8,128)S(1)}, f32[2,128,128]{2,1,0:T(8,128)S(1)}, u32[]{:S(2)}, u32[]{:S(2)}) collective-permute-start(f32[2,128,128]{2,1,0:T(8,128)S(1)} %collective-permute-done.5.upper_ref), channel_id=1, source_target_pairs={{2,0},{4,2},{6,4},{8,6},{10,8},{12,10},{14,12},{16,14},{18,16},{20... | collective-permute-start | bytes 393224 | tf_op jit(solution)/shard_map/ppermute | solution.py:23
  31.1 7.3 %collective-permute-start.9 = (f32[2,128,128]{2,1,0:T(8,128)S(1)}, f32[2,128,128]{2,1,0:T(8,128)S(1)}, u32[]{:S(2)}, u32[]{:S(2)}) collective-permute-start(f32[2,128,128]{2,1,0:T(8,128)S(1)} %get-tuple-element.51), channel_id=1, source_target_pairs={{30,0},{0,2},{2,4},{4,6},{6,8},{8,10},{10,12},{12,14},{14,16},{16,... | collective-permute-start | bytes 393224 | tf_op jit(solution)/shard_map/ppermute | solution.py:23
  31.2 13.7 %collective-permute-start.8 = (f32[2,128,256]{2,1,0:T(8,128)S(1)}, f32[2,128,256]{2,1,0:T(8,128)S(1)}, u32[]{:S(2)}, u32[]{:S(2)}) collective-permute-start(f32[2,128,256]{2,1,0:T(8,128)S(1)} %get-tuple-element.49), channel_id=1, source_target_pairs={{30,0},{0,2},{2,4},{4,6},{6,8},{8,10},{10,12},{12,14},{14,16},{16,... | collective-permute-start | bytes 786440 | tf_op jit(solution)/shard_map/ppermute | solution.py:23
  31.2 11.3 %collective-permute-start.13 = (f32[2,128,128]{2,1,0:T(8,128)S(1)}, f32[2,128,128]{2,1,0:T(8,128)S(1)}, u32[]{:S(2)}, u32[]{:S(2)}) collective-permute-start(f32[2,128,128]{2,1,0:T(8,128)S(1)} %get-tuple-element.57), channel_id=1, source_target_pairs={{30,0},{0,2},{2,4},{4,6},{6,8},{8,10},{10,12},{12,14},{14,16},{16,... | collective-permute-start | bytes 393224 | tf_op jit(solution)/shard_map/ppermute | solution.py:23
  32.6 11.6 %collective-permute-start.11 = (f32[2,128,128]{2,1,0:T(8,128)S(1)}, f32[2,128,128]{2,1,0:T(8,128)S(1)}, u32[]{:S(2)}, u32[]{:S(2)}) collective-permute-start(f32[2,128,128]{2,1,0:T(8,128)S(1)} %get-tuple-element.52), channel_id=1, source_target_pairs={{1,0},{0,1},{3,2},{2,3},{5,4},{4,5},{7,6},{6,7},{9,8},{8,9},{11,10... | collective-permute-start | bytes 393224 | tf_op jit(solution)/shard_map/ppermute | solution.py:23
  34.1 15.1 %collective-permute-start.12 = (f32[2,128,256]{2,1,0:T(8,128)S(1)}, f32[2,128,256]{2,1,0:T(8,128)S(1)}, u32[]{:S(2)}, u32[]{:S(2)}) collective-permute-start(f32[2,128,256]{2,1,0:T(8,128)S(1)} %get-tuple-element.55), channel_id=1, source_target_pairs={{30,0},{0,2},{2,4},{4,6},{6,8},{8,10},{10,12},{12,14},{14,16},{16,... | collective-permute-start | bytes 786440 | tf_op jit(solution)/shard_map/ppermute | solution.py:23
  38.4 6.4 %collective-permute-start.10 = (f32[2,128,128]{2,1,0:T(8,128)S(1)}, f32[2,128,128]{2,1,0:T(8,128)S(1)}, u32[]{:S(2)}, u32[]{:S(2)}) collective-permute-start(f32[2,128,128]{2,1,0:T(8,128)S(1)} %add.12), channel_id=1, source_target_pairs={{1,0},{0,1},{3,2},{2,3},{5,4},{4,5},{7,6},{6,7},{9,8},{8,9},{11,10... | collective-permute-start | bytes 393224 | tf_op jit(solution)/shard_map/ppermute | solution.py:23
  42.6 5.0 %collective-permute-start.15 = (f32[2,128,128]{2,1,0:T(8,128)S(1)}, f32[2,128,128]{2,1,0:T(8,128)S(1)}, u32[]{:S(2)}, u32[]{:S(2)}) collective-permute-start(f32[2,128,128]{2,1,0:T(8,128)S(1)} %get-tuple-element.58), channel_id=1, source_target_pairs={{1,0},{0,1},{3,2},{2,3},{5,4},{4,5},{7,6},{6,7},{9,8},{8,9},{11,10... | collective-permute-start | bytes 393224 | tf_op jit(solution)/shard_map/ppermute | solution.py:23
  44.1 5.0 %collective-permute-start.14 = (f32[2,128,128]{2,1,0:T(8,128)S(1)}, f32[2,128,128]{2,1,0:T(8,128)S(1)}, u32[]{:S(2)}, u32[]{:S(2)}) collective-permute-start(f32[2,128,128]{2,1,0:T(8,128)S(1)} %add.13), channel_id=1, source_target_pairs={{1,0},{0,1},{3,2},{2,3},{5,4},{4,5},{7,6},{6,7},{9,8},{8,9},{11,10... | collective-permute-start | bytes 393224 | tf_op jit(solution)/shard_map/ppermute | solution.py:23
  45.0 6.4 %collective-permute-start.21 = (f32[2,128,128]{2,1,0:T(8,128)S(1)}, f32[2,128,128]{2,1,0:T(8,128)S(1)}, u32[]{:S(2)}, u32[]{:S(2)}) collective-permute-start(f32[2,128,128]{2,1,0:T(8,128)S(1)} %get-tuple-element.64), channel_id=1, source_target_pairs={{1,0},{0,1},{3,2},{2,3},{5,4},{4,5},{7,6},{6,7},{9,8},{8,9},{11,10... | collective-permute-start | bytes 393224 | tf_op jit(solution)/shard_map/ppermute | solution.py:23
  46.5 13.2 %collective-permute-start.20 = (f32[2,128,256]{2,1,0:T(8,128)S(1)}, f32[2,128,256]{2,1,0:T(8,128)S(1)}, u32[]{:S(2)}, u32[]{:S(2)}) collective-permute-start(f32[2,128,256]{2,1,0:T(8,128)S(1)} %get-tuple-element.63), channel_id=1, source_target_pairs={{2,0},{4,2},{6,4},{8,6},{10,8},{12,10},{14,12},{16,14},{18,16},{20... | collective-permute-start | bytes 786440 | tf_op jit(solution)/shard_map/ppermute | solution.py:23
  49.3 5.4 %collective-permute-start.17 = (f32[2,128,128]{2,1,0:T(8,128)S(1)}, f32[2,128,128]{2,1,0:T(8,128)S(1)}, u32[]{:S(2)}, u32[]{:S(2)}) collective-permute-start(f32[2,128,128]{2,1,0:T(8,128)S(1)} %get-tuple-element.61), channel_id=1, source_target_pairs={{1,0},{0,1},{3,2},{2,3},{5,4},{4,5},{7,6},{6,7},{9,8},{8,9},{11,10... | collective-permute-start | bytes 393224 | tf_op jit(solution)/shard_map/ppermute | solution.py:23
  50.8 11.7 %collective-permute-start.16 = (f32[2,128,256]{2,1,0:T(8,128)S(1)}, f32[2,128,256]{2,1,0:T(8,128)S(1)}, u32[]{:S(2)}, u32[]{:S(2)}) collective-permute-start(f32[2,128,256]{2,1,0:T(8,128)S(1)} %get-tuple-element.60), channel_id=1, source_target_pairs={{2,0},{4,2},{6,4},{8,6},{10,8},{12,10},{14,12},{16,14},{18,16},{20... | collective-permute-start | bytes 786440 | tf_op jit(solution)/shard_map/ppermute | solution.py:23
  50.8 6.7 %collective-permute-start.22 = (f32[2,128,128]{2,1,0:T(8,128)S(1)}, f32[2,128,128]{2,1,0:T(8,128)S(1)}, u32[]{:S(2)}, u32[]{:S(2)}) collective-permute-start(f32[2,128,128]{2,1,0:T(8,128)S(1)} %get-tuple-element.65), channel_id=1, source_target_pairs={{1,0},{0,1},{3,2},{2,3},{5,4},{4,5},{7,6},{6,7},{9,8},{8,9},{11,10... | collective-permute-start | bytes 393224 | tf_op jit(solution)/shard_map/ppermute | solution.py:23
  51.4 8.4 %collective-permute-start.23 = (f32[2,128,128]{2,1,0:T(8,128)S(1)}, f32[2,128,128]{2,1,0:T(8,128)S(1)}, u32[]{:S(2)}, u32[]{:S(2)}) collective-permute-start(f32[2,128,128]{2,1,0:T(8,128)S(1)} %collective-permute-done.21.upper_ref), channel_id=1, source_target_pairs={{2,0},{4,2},{6,4},{8,6},{10,8},{12,10},{14,12},{16,14},{18,16},{20... | collective-permute-start | bytes 393224 | tf_op jit(solution)/shard_map/ppermute | solution.py:23
  54.7 7.8 %collective-permute-start.18 = (f32[2,128,128]{2,1,0:T(8,128)S(1)}, f32[2,128,128]{2,1,0:T(8,128)S(1)}, u32[]{:S(2)}, u32[]{:S(2)}) collective-permute-start(f32[2,128,128]{2,1,0:T(8,128)S(1)} %get-tuple-element.62), channel_id=1, source_target_pairs={{1,0},{0,1},{3,2},{2,3},{5,4},{4,5},{7,6},{6,7},{9,8},{8,9},{11,10... | collective-permute-start | bytes 393224 | tf_op jit(solution)/shard_map/ppermute | solution.py:23
  57.5 5.0 %collective-permute-start.19 = (f32[2,128,128]{2,1,0:T(8,128)S(1)}, f32[2,128,128]{2,1,0:T(8,128)S(1)}, u32[]{:S(2)}, u32[]{:S(2)}) collective-permute-start(f32[2,128,128]{2,1,0:T(8,128)S(1)} %collective-permute-done.17.upper_ref), channel_id=1, source_target_pairs={{2,0},{4,2},{6,4},{8,6},{10,8},{12,10},{14,12},{16,14},{18,16},{20... | collective-permute-start | bytes 393224 | tf_op jit(solution)/shard_map/ppermute | solution.py:23
  65.7 7.3 %collective-permute-start.29 = (f32[2,128,128]{2,1,0:T(8,128)S(1)}, f32[2,128,128]{2,1,0:T(8,128)S(1)}, u32[]{:S(2)}, u32[]{:S(2)}) collective-permute-start(f32[2,128,128]{2,1,0:T(8,128)S(1)} %get-tuple-element.75), channel_id=1, source_target_pairs={{30,0},{0,2},{2,4},{4,6},{6,8},{8,10},{10,12},{12,14},{14,16},{16,... | collective-permute-start | bytes 393224 | tf_op jit(solution)/shard_map/ppermute | solution.py:23
  68.9 7.1 %collective-permute-start.25 = (f32[2,128,128]{2,1,0:T(8,128)S(1)}, f32[2,128,128]{2,1,0:T(8,128)S(1)}, u32[]{:S(2)}, u32[]{:S(2)}) collective-permute-start(f32[2,128,128]{2,1,0:T(8,128)S(1)} %get-tuple-element.70), channel_id=1, source_target_pairs={{30,0},{0,2},{2,4},{4,6},{6,8},{8,10},{10,12},{12,14},{14,16},{16,... | collective-permute-start | bytes 393224 | tf_op jit(solution)/shard_map/ppermute | solution.py:23
  68.9 7.7 %collective-permute-start.31 = (f32[2,128,128]{2,1,0:T(8,128)S(1)}, f32[2,128,128]{2,1,0:T(8,128)S(1)}, u32[]{:S(2)}, u32[]{:S(2)}) collective-permute-start(f32[2,128,128]{2,1,0:T(8,128)S(1)} %get-tuple-element.76), channel_id=1, source_target_pairs={{1,0},{0,1},{3,2},{2,3},{5,4},{4,5},{7,6},{6,7},{9,8},{8,9},{11,10... | collective-permute-start | bytes 393224 | tf_op jit(solution)/shard_map/ppermute | solution.py:23
  69.6 12.2 %collective-permute-start.28 = (f32[2,128,256]{2,1,0:T(8,128)S(1)}, f32[2,128,256]{2,1,0:T(8,128)S(1)}, u32[]{:S(2)}, u32[]{:S(2)}) collective-permute-start(f32[2,128,256]{2,1,0:T(8,128)S(1)} %get-tuple-element.73), channel_id=1, source_target_pairs={{30,0},{0,2},{2,4},{4,6},{6,8},{8,10},{10,12},{12,14},{14,16},{16,... | collective-permute-start | bytes 786440 | tf_op jit(solution)/shard_map/ppermute | solution.py:23
  70.9 12.4 %collective-permute-start.24 = (f32[2,128,256]{2,1,0:T(8,128)S(1)}, f32[2,128,256]{2,1,0:T(8,128)S(1)}, u32[]{:S(2)}, u32[]{:S(2)}) collective-permute-start(f32[2,128,256]{2,1,0:T(8,128)S(1)} %get-tuple-element.68), channel_id=1, source_target_pairs={{30,0},{0,2},{2,4},{4,6},{6,8},{8,10},{10,12},{12,14},{14,16},{16,... | collective-permute-start | bytes 786440 | tf_op jit(solution)/shard_map/ppermute | solution.py:23
  73.0 6.4 %collective-permute-start.27 = (f32[2,128,128]{2,1,0:T(8,128)S(1)}, f32[2,128,128]{2,1,0:T(8,128)S(1)}, u32[]{:S(2)}, u32[]{:S(2)}) collective-permute-start(f32[2,128,128]{2,1,0:T(8,128)S(1)} %get-tuple-element.71), channel_id=1, source_target_pairs={{1,0},{0,1},{3,2},{2,3},{5,4},{4,5},{7,6},{6,7},{9,8},{8,9},{11,10... | collective-permute-start | bytes 393224 | tf_op jit(solution)/shard_map/ppermute | solution.py:23
  76.0 5.8 %collective-permute-start.30 = (f32[2,128,128]{2,1,0:T(8,128)S(1)}, f32[2,128,128]{2,1,0:T(8,128)S(1)}, u32[]{:S(2)}, u32[]{:S(2)}) collective-permute-start(f32[2,128,128]{2,1,0:T(8,128)S(1)} %add.15), channel_id=1, source_target_pairs={{1,0},{0,1},{3,2},{2,3},{5,4},{4,5},{7,6},{6,7},{9,8},{8,9},{11,10... | collective-permute-start | bytes 393224 | tf_op jit(solution)/shard_map/ppermute | solution.py:23
  76.6 6.6 %collective-permute-start.26 = (f32[2,128,128]{2,1,0:T(8,128)S(1)}, f32[2,128,128]{2,1,0:T(8,128)S(1)}, u32[]{:S(2)}, u32[]{:S(2)}) collective-permute-start(f32[2,128,128]{2,1,0:T(8,128)S(1)} %add.14), channel_id=1, source_target_pairs={{1,0},{0,1},{3,2},{2,3},{5,4},{4,5},{7,6},{6,7},{9,8},{8,9},{11,10... | collective-permute-start | bytes 393224 | tf_op jit(solution)/shard_map/ppermute | solution.py:23
  (12 other events, 78.9 us)

commit v2 on v1

v2 whole, which is shorter than its diff:
```python
import functools
import math

import jax
import jax.numpy as jnp
import ml_dtypes
import numpy as np
from jax import lax
from jax.experimental import pallas as pl
from jax.experimental.pallas import tpu as pltpu
from jax.sharding import PartitionSpec as P

ITERS = 2
LANES = 128

step_size = 0.02
floor_amp = 0.5


def from_behind(block, axis, distance):
    devices = range(lax.axis_size(axis))
    route = [((i - distance) % len(devices), i) for i in devices]
    return lax.ppermute(block, axis, route)


def two_parts(value):
    high = value.astype(ml_dtypes.bfloat16)
    low = (value - high.astype(np.float64)).astype(ml_dtypes.bfloat16)
    return high, low


def dft_operands(width):
    index = np.arange(width)
    angle = (index[:, None] * index[None, :] % width) * (2.0 * math.pi / width)
    real = np.cos(angle) / math.sqrt(width)
    imag = -np.sin(angle) / math.sqrt(width)
    right = np.block([[real, imag], [-imag, real]])
    right_high, right_low = two_parts(right)
    left_high, left_low = two_parts(right.T)
    return np.stack([right_high, right_low, left_high, left_low])


def split(value):
    high = value.astype(jnp.bfloat16)
    low = (value - high.astype(jnp.float32)).astype(jnp.bfloat16)
    return high, low


def rows_of(j, width):
    return slice(j * width, (j + 1) * width)


def put(a_ref, j, width, real, imag):
    real_high, real_low = split(real)
    imag_high, imag_low = split(imag)
    rows = rows_of(j, width)
    a_ref[rows, 0:width] = real_high
    a_ref[rows, width:2 * width] = imag_high
    a_ref[rows, 2 * width:3 * width] = real_low
    a_ref[rows, 3 * width:4 * width] = imag_low


def product(left, right):
    return jnp.dot(left, right, preferred_element_type=jnp.float32)


def transform(a_ref, b_ref, table_ref, spots, width):
    both = 2 * width
    half = product(a_ref[:, :both], table_ref[0]) + product(a_ref[:, both:], table_ref[0])
    half += product(a_ref[:, :both], table_ref[1])
    for j in range(spots):
        rows = rows_of(j, width)
        real_high, real_low = split(half[rows, :width])
        imag_high, imag_low = split(half[rows, width:])
        b_ref[0:width, rows] = real_high
        b_ref[width:2 * width, rows] = imag_high
        b_ref[2 * width:3 * width, rows] = real_low
        b_ref[3 * width:4 * width, rows] = imag_low
    full = product(table_ref[2], b_ref[:both, :]) + product(table_ref[2], b_ref[both:, :])
    full += product(table_ref[3], b_ref[:both, :])
    return [
        (full[:width, rows_of(j, width)], full[width:, rows_of(j, width)]) for j in range(spots)
    ]


def fill_ext(ext_ref, tile_ref, below_ref, upper_ref, lower_ref, corner_ref, width):
    tile_px = tile_ref.shape[1]
    blocks = tile_px // LANES
    for c in range(2):
        for b in range(blocks):
            lanes = slice(b * LANES, (b + 1) * LANES)
            ext_ref[c, b, :tile_px, :] = tile_ref[c, :, lanes]
            ext_ref[c, b, tile_px:, :] = below_ref[c, :, lanes]
        ext_ref[c, blocks, :width, :] = upper_ref[c]
        ext_ref[c, blocks, width:tile_px, :] = lower_ref[c]
        ext_ref[c, blocks, tile_px:, :] = corner_ref[c]


def place(scalar_ref, j):
    col = scalar_ref[2 * j + 1]
    return scalar_ref[2 * j], col // LANES, col % LANES


def window(ext_ref, c, spot, width, lane):
    row, block, shift = spot
    near = ext_ref[c, block, pl.ds(row, width), :]
    far = ext_ref[c, block + 1, pl.ds(row, width), :]
    return pltpu.roll(jnp.where(lane >= shift, near, far), LANES - shift, 1)


def scatter(grad_ref, c, spot, width, lane, used, update):
    row, block, shift = spot
    turned = pltpu.roll(jnp.where(used, update, 0.0), shift, 1)
    near = lane >= shift
    grad_ref[c, block, pl.ds(row, width), :] += jnp.where(near, turned, 0.0)
    grad_ref[c, block + 1, pl.ds(row, width), :] += jnp.where(near, 0.0, turned)


def emit(grad_ref, own_ref, down_ref, upper_ref, lower_ref, diag_ref, width):
    tile_px = own_ref.shape[1]
    blocks = tile_px // LANES
    for c in range(2):
        for b in range(blocks):
            lanes = slice(b * LANES, (b + 1) * LANES)
            own_ref[c, :, lanes] = grad_ref[c, b, :tile_px, :]
            down_ref[c, :, lanes] = grad_ref[c, b, tile_px:, :]
        upper_ref[c] = grad_ref[c, blocks, :width, :]
        lower_ref[c] = grad_ref[c, blocks, width:tile_px, :]
        diag_ref[c] = grad_ref[c, blocks, tile_px:, :]


def lanes_of(width):
    return lax.broadcasted_iota(jnp.int32, (width, LANES), 1)


def views(refs, s):
    picked = []
    for ref in refs:
        if isinstance(ref, (list, tuple)):
            picked.append(ref[s])
        elif len(ref.shape) == 4:
            picked.append(ref.at[s])
        else:
            picked.append(ref.at[pl.ds(2 * s, 2)])
    return picked


def paired(refs, kinds):
    refs = list(refs)
    return [refs.pop(0) if kind == 1 else (refs.pop(0), refs.pop(0)) for kind in kinds]


def fetch(far_refs, near_refs, sems):
    copies = [
        pltpu.make_async_copy(far, near, sems.at[k])
        for k, (far, near) in enumerate(zip(far_refs, near_refs))
    ]
    for copy in copies:
        copy.start()
    return copies


def wave_kernel(*refs, spots, width, kinds):
    count = 1 + sum(kinds)
    scalar_ref, halo_refs, rest = refs[0], paired(refs[1:count], kinds), refs[count:]
    prop_ref, *far = rest[:4]
    own_ref, down_ref, up_out_ref, low_out_ref, diag_ref, back_ref = rest[4:10]
    ext_ref, win_ref, moved_ref, a_ref, b_ref, *near, sems = rest[10:]
    fetches = fetch(far, near, sems)
    probe_ref, amp_ref, table_ref = near
    lane = lanes_of(width)
    total = scalar_ref[2 * spots]
    spot_list = [place(scalar_ref, j) for j in range(spots)]
    fill_ext(ext_ref, *views(halo_refs, 0), width)
    for fetched in fetches:
        fetched.wait()
    for j in range(spots):
        real = window(ext_ref, 0, spot_list[j], width, lane)
        imag = window(ext_ref, 1, spot_list[j], width, lane)
        put(
            a_ref, j, width,
            probe_ref[0] * real - probe_ref[1] * imag,
            probe_ref[0] * imag + probe_ref[1] * real,
        )
    fill_ext(ext_ref, *views(halo_refs, 1), width)
    for j in range(spots):
        win_ref[j, 0] = window(ext_ref, 0, spot_list[j], width, lane)
        win_ref[j, 1] = window(ext_ref, 1, spot_list[j], width, lane)
    for j, (real, imag) in enumerate(transform(a_ref, b_ref, table_ref, spots, width)):
        put(
            a_ref, j, width,
            prop_ref[0] * real - prop_ref[1] * imag,
            -(prop_ref[0] * imag + prop_ref[1] * real),
        )
    for j, (real, negative) in enumerate(transform(a_ref, b_ref, table_ref, spots, width)):
        imag = -negative
        moved_ref[j, 0] = real
        moved_ref[j, 1] = imag
        put(
            a_ref, j, width,
            real * win_ref[j, 0] - imag * win_ref[j, 1],
            real * win_ref[j, 1] + imag * win_ref[j, 0],
        )
    ext_ref[...] = jnp.zeros(ext_ref.shape, jnp.float32)
    for j, (real, imag) in enumerate(transform(a_ref, b_ref, table_ref, spots, width)):
        measured = amp_ref[scalar_ref[2 * spots + 1 + j]]
        power = jnp.maximum(real * real + imag * imag, floor_amp * floor_amp)
        factor = 1.0 - measured * lax.rsqrt(power)
        put(a_ref, j, width, real * factor, -(imag * factor))
    for j, (real, negative) in enumerate(transform(a_ref, b_ref, table_ref, spots, width)):
        imag = -negative
        used = j < total
        scatter(ext_ref, 0, spot_list[j], width, lane, used, moved_ref[j, 0] * real + moved_ref[j, 1] * imag)
        scatter(ext_ref, 1, spot_list[j], width, lane, used, moved_ref[j, 0] * imag - moved_ref[j, 1] * real)
        back_ref[j, 0] = win_ref[j, 0] * real + win_ref[j, 1] * imag
        back_ref[j, 1] = win_ref[j, 0] * imag - win_ref[j, 1] * real
    emit(ext_ref, own_ref, down_ref, up_out_ref, low_out_ref, diag_ref, width)


def backward_kernel(
    scalar_ref, back_ref, other_down_ref, prop_ref, probe_far_ref, table_far_ref,
    own_ref, down_ref, up_out_ref, low_out_ref, diag_ref,
    ext_ref, a_ref, b_ref, probe_ref, table_ref, sems, *, spots, width,
):
    fetches = fetch((probe_far_ref, table_far_ref), (probe_ref, table_ref), sems)
    lane = lanes_of(width)
    total = scalar_ref[2 * spots]
    for j in range(spots):
        put(a_ref, j, width, back_ref[j, 0], back_ref[j, 1])
    ext_ref[...] = jnp.zeros(ext_ref.shape, jnp.float32)
    down_ref[2:] = other_down_ref[...]
    for fetched in fetches:
        fetched.wait()
    for j, (real, imag) in enumerate(transform(a_ref, b_ref, table_ref, spots, width)):
        put(
            a_ref, j, width,
            prop_ref[0] * real + prop_ref[1] * imag,
            -(prop_ref[0] * imag - prop_ref[1] * real),
        )
    for j, (real, negative) in enumerate(transform(a_ref, b_ref, table_ref, spots, width)):
        imag = -negative
        spot = place(scalar_ref, j)
        used = j < total
        scatter(ext_ref, 0, spot, width, lane, used, probe_ref[0] * real + probe_ref[1] * imag)
        scatter(ext_ref, 1, spot, width, lane, used, probe_ref[0] * imag - probe_ref[1] * real)
    emit(ext_ref, own_ref, down_ref, up_out_ref, low_out_ref, diag_ref, width)


def folded(tile_ref, own_ref, above_ref, upper_ref, lower_ref, c, width):
    tile_px = own_ref.shape[1]
    top, low = slice(0, width), slice(width, tile_px)
    left, rest = slice(0, width), slice(width, tile_px)
    yield top, left, tile_ref[c, top, left] - step_size * (
        own_ref[c, top, left] + above_ref[c, :, left] + upper_ref[c]
    )
    yield top, rest, tile_ref[c, top, rest] - step_size * (own_ref[c, top, rest] + above_ref[c, :, rest])
    yield low, left, tile_ref[c, low, left] - step_size * (own_ref[c, low, left] + lower_ref[c])
    yield low, rest, tile_ref[c, low, rest] - step_size * own_ref[c, low, rest]


def update_second_kernel(
    tile_ref, own_ref, above_ref, upper_ref, lower_ref, new_ref, left_up_ref, *, width,
):
    tile_ref, above_ref = views((tile_ref, above_ref), 1)
    for c in range(2):
        for k, (rows, lanes, value) in enumerate(
            folded(tile_ref, own_ref, above_ref, upper_ref, lower_ref, c, width)
        ):
            new_ref[c, rows, lanes] = value
            if k == 0:
                left_up_ref[c] = value


def update_first_kernel(
    tile_ref, own_ref, above_ref, upper_ref, lower_ref, second_ref,
    new_ref, left_up_ref, left_low_ref, top_ref, *, width,
):
    tile_ref, above_ref = views((tile_ref, above_ref), 0)
    for c in range(2):
        for k, (rows, lanes, value) in enumerate(
            folded(tile_ref, own_ref, above_ref, upper_ref, lower_ref, c, width)
        ):
            new_ref[c, rows, lanes] = value
            if k < 2:
                top_ref[c, :, lanes] = value
            if k == 0:
                left_up_ref[c] = value
            if k == 2:
                left_low_ref[c] = value
        top_ref[2 + c] = second_ref[c, :width, :]
        left_low_ref[2 + c] = second_ref[c, width:, :width]


def finish_kernel(first_ref, second_ref, own_one, own_two, above_ref, up_one, up_two, low_one, low_two, out_ref, *, width):
    refs = ((first_ref, second_ref), (own_one, own_two), above_ref, (up_one, up_two), (low_one, low_two))
    for s in (1, 0):
        for c in range(2):
            for rows, lanes, value in folded(*views(refs, s), c, width):
                out_ref[s, c, rows, lanes] = value


F32 = functools.partial(jax.ShapeDtypeStruct, dtype=jnp.float32)
SMEM = pl.BlockSpec(memory_space=pltpu.SMEM)
VMEM = pl.BlockSpec(memory_space=pltpu.VMEM)
LIMIT = pltpu.CompilerParams(vmem_limit_bytes=16 * 1024 * 1024)


FAR = pl.BlockSpec(memory_space=pltpu.MemorySpace.HBM)


def call(kernel, scalars, arrays, outs, scratch, far=(), **static):
    fetched = [pltpu.VMEM(x.shape, x.dtype) for x in far]
    if far:
        fetched.append(pltpu.SemaphoreType.DMA((len(far),)))
    return pl.pallas_call(
        functools.partial(kernel, **static),
        in_specs=[SMEM] * len(scalars) + [VMEM] * len(arrays) + [FAR] * len(far),
        out_specs=[VMEM] * len(outs),
        out_shape=outs,
        scratch_shapes=[*scratch, *fetched],
        compiler_params=LIMIT,
    )(*scalars, *arrays, *far)


def pack_kernel(whole_ref, up_ref, low_ref, top_ref, sems, *, width):
    tile_px = whole_ref.shape[2]
    left = pl.ds(0, width)
    copies = []
    for s in range(2):
        both = pl.ds(2 * s, 2)
        copies.append((whole_ref.at[s, :, pl.ds(0, width), left], up_ref.at[both]))
        copies.append((whole_ref.at[s, :, pl.ds(width, tile_px - width), left], low_ref.at[both]))
        copies.append((whole_ref.at[s, :, pl.ds(0, width), :], top_ref.at[both]))
    copies = [pltpu.make_async_copy(a, b, sems.at[k]) for k, (a, b) in enumerate(copies)]
    for copy in copies:
        copy.start()
    for copy in copies:
        copy.wait()


def in_hbm(array):
    return pltpu.with_memory_space_constraint(array, pltpu.MemorySpace.HBM)


def body(
    specimen_slices,
    illumination_probe,
    propagation_phase,
    amplitudes,
    positions,
    counts,
    measurement_index,
):
    tile_px = specimen_slices.shape[2]
    width = illumination_probe.shape[1]
    spots = positions.shape[2]
    ext = tile_px + width
    table = in_hbm(jnp.asarray(dft_operands(width)))
    probe = in_hbm(illumination_probe)
    prop = jnp.stack([jnp.cos(propagation_phase), jnp.sin(propagation_phase)])
    scalars = (jnp.concatenate([positions.reshape(-1), counts.reshape(-1), measurement_index.reshape(-1)]),)
    measured = in_hbm(amplitudes[0, 0])
    static = dict(spots=spots, width=width)
    ext_space = pltpu.VMEM((2, ext // LANES, ext, LANES), jnp.float32)
    work = [
        pltpu.VMEM((spots * width, 4 * width), jnp.bfloat16),
        pltpu.VMEM((4 * width, spots * width), jnp.bfloat16),
    ]
    wave = F32((spots, 2, width, width))
    square = F32((2, width, width))
    squares = F32((4, width, width))
    whole = F32((2, tile_px, tile_px))
    strip = F32((2, width, tile_px))
    strips = F32((4, width, tile_px))
    wave_space = pltpu.VMEM((spots, 2, width, width), jnp.float32)

    def add_and_send(block, corner):
        return from_behind(block + corner, "col", 1)

    left_up, left_low, top = pl.pallas_call(
        functools.partial(pack_kernel, width=width),
        in_specs=[FAR],
        out_specs=[VMEM] * 3,
        out_shape=[squares, squares, strips],
        scratch_shapes=[pltpu.SemaphoreType.DMA((6,))],
        compiler_params=LIMIT,
        name="pack",
    )(in_hbm(specimen_slices))
    upper = from_behind(left_up, "col", -1)
    lower = from_behind(left_low, "col", -1)
    below = from_behind(top, "row", -1)
    corner = from_behind(upper, "row", -1)
    halo, kinds = [specimen_slices, below, upper, lower, corner], (1, 1, 1, 1, 1)
    tiles = (specimen_slices,)
    for i in range(ITERS):
        own_two, down_two, up_two, low_two, diag_two, back = call(
            wave_kernel, scalars, (*halo, prop),
            [whole, strip, square, square, square, wave],
            [ext_space, wave_space, wave_space, *work],
            far=(probe, measured, table), kinds=kinds, **static,
        )
        corner_two = from_behind(diag_two, "row", 1)
        low_two = from_behind(low_two, "col", 1)
        own_one, down, up_one, low_one, diag_one = call(
            backward_kernel, scalars, (back, down_two, prop),
            [whole, strips, square, square, square], [ext_space, *work],
            far=(probe, table), **static,
        )
        low_one = from_behind(low_one, "col", 1)
        corner_one = from_behind(diag_one, "row", 1)
        above = from_behind(down, "row", 1)
        up_two = add_and_send(up_two, corner_two)
        up_one = add_and_send(up_one, corner_one)
        if i + 1 < ITERS:
            second, left_up_two = call(
                update_second_kernel, (), (tiles[-1], own_two, above, up_two, low_two),
                [whole, square], [], width=width,
            )
            upper_two = from_behind(left_up_two, "col", -1)
            first, left_up_one, left_low, top = call(
                update_first_kernel, (), (tiles[0], own_one, above, up_one, low_one, second),
                [whole, square, squares, strips], [], width=width,
            )
            upper_one = from_behind(left_up_one, "col", -1)
            lower = from_behind(left_low, "col", -1)
            below = from_behind(top, "row", -1)
            corner_one = from_behind(upper_one, "row", -1)
            corner_two = from_behind(upper_two, "row", -1)
            tiles = (first, second)
            halo = [*tiles, below, upper_one, upper_two, lower, corner_one, corner_two]
            kinds = (2, 1, 2, 1, 2)
        else:
            (updated,) = call(
                finish_kernel, (),
                (*tiles, own_one, own_two, above, up_one, up_two, low_one, low_two),
                [F32(specimen_slices.shape)], [], width=width,
            )
    return updated


def solution(mesh):
    placed = (
        P(None, None, "row", "col"),
        P(),
        P(),
        P("row", "col", None, None, None),
        P("row", "col", None, None),
        P("row", "col"),
        P("row", "col", None),
    )

    return jax.shard_map(
        body, mesh=mesh, in_specs=placed, out_specs=P(None, None, "row", "col"), check_vma=False
    )
```

time: 84.7 us -> 94.7 us (1.12)
  waiting for transfers between devices: 22.1 us -> 40.9 us
  starting transfers between devices: 36.8 us -> 27.4 us
  Pallas kernels: 19.1 us -> 23.2 us
  local copies, waits for them, and re-layouts: 5.27 us -> 1.93 us
    ppermute x32 -> x24, waiting for transfers between devices: 22.1 us -> 40.9 us  [from_behind(): return lax.ppermute(block, axis, route)]
    ppermute x32 -> x24, starting transfers between devices: 36.8 us -> 27.4 us  [from_behind(): return lax.ppermute(block, axis, route)]
    unnamed x25 -> x7, local copies, waits for them, and re-layouts: 4.11 us -> 0.77 us
    pallas_call x9 -> x7, Pallas kernels: 19 us -> 21.9 us  [call(): pl.pallas_call(functools.partial(kernel, **static), in_specs=[SMEM] * len...]
    pallas_call x1, Pallas kernels: 0.14 us -> 1.38 us  [body(): pl.pallas_call(functools.partial(pack_kernel, width=width), in_specs=[FAR...]
  transfers between devices with their start and end apart: 32 -> 24, of which waited for: 13 -> 13; matrix products, arithmetic and copies ran while one was open for 2% -> 1% of each run, Pallas kernels for 10% -> 0%
where the time goes in v2:
time: 94.7 us; the launch traced here: 94.4 us
  waiting for transfers between devices  40.9 us (43%)
  starting transfers between devices  27.4 us (29%)
  Pallas kernels  23.2 us (24%)
  local copies, waits for them, and re-layouts  1.93 us (2%)
    ppermute x24, waiting for transfers between devices, from_behind(): return lax.ppermute(block, axis, route)  40.9 us
    ppermute x24, starting transfers between devices, from_behind(): return lax.ppermute(block, axis, route)  27.4 us
    pallas_call x7, Pallas kernels, call(): pl.pallas_call(functools.partial(kernel, **static), in_specs=[SMEM] * len...  21.9 us
  transfers between devices with their start and end apart: 24, of which 13 were waited for; matrix products, arithmetic and copies ran while one was open for 1% of the time, Pallas kernels for 0%

profile of v2, /device:TPU:0, one launch (start us, length us, event | category | flops | bytes accessed | tf_op | source)
XLA Modules:
  0.0 94.4 jit_solution(11436499576300288795)
XLA Ops:
  0.0 1.4 %pack.1 = (f32[4,128,128]{2,1,0:T(8,128)S(1)}, f32[4,128,128]{2,1,0:T(8,128)S(1)}, f32[4,128,256]{2,1,0:T(8,128)S(1)}) custom-call(f32[2,2,256,256]{3,2,1,0:T(8,128)} %tile_ref.3), custom_call_target="tpu_custom_call" | custom-call | tf_op jit(solution)/shard_map/pack/pallas_call | solution.py:380
  1.4 3.0 %collective-permute-start.1 = (f32[4,128,128]{2,1,0:T(8,128)S(1)}, f32[4,128,128]{2,1,0:T(8,128)S(1)}, u32[]{:S(2)}, u32[]{:S(2)}) collective-permute-start(f32[4,128,128]{2,1,0:T(8,128)S(1)} %get-tuple-element.37), channel_id=1, source_target_pairs={{1,0},{0,1},{3,2},{2,3},{5,4},{4,5},{7,6},{6,7},{9,8},{8,9},{11,10... | collective-permute-start | bytes 786440 | tf_op jit(solution)/shard_map/ppermute | solution.py:23
  4.4 3.7 %collective-permute-start = (f32[4,128,256]{2,1,0:T(8,128)S(1)}, f32[4,128,256]{2,1,0:T(8,128)S(1)}, u32[]{:S(2)}, u32[]{:S(2)}) collective-permute-start(f32[4,128,256]{2,1,0:T(8,128)S(1)} %get-tuple-element.36), channel_id=1, source_target_pairs={{2,0},{4,2},{6,4},{8,6},{10,8},{12,10},{14,12},{16,14},{18,16},{20... | collective-permute-start | bytes 1572872 | tf_op jit(solution)/shard_map/ppermute | solution.py:23
  8.7 2.9 %collective-permute-done.1.refs_3_ = f32[4,128,128]{2,1,0:T(8,128)S(1)} collective-permute-done((f32[4,128,128]{2,1,0:T(8,128)S(1)}, f32[4,128,128]{2,1,0:T(8,128)S(1)}, u32[]{:S(2)}, u32[]{:S(2)}) %collective-permute-start.1) | collective-permute-done | bytes 262176 | tf_op jit(solution)/shard_map/ppermute | solution.py:23
  11.6 2.5 %collective-permute-start.3 = (f32[4,128,128]{2,1,0:T(8,128)S(1)}, f32[4,128,128]{2,1,0:T(8,128)S(1)}, u32[]{:S(2)}, u32[]{:S(2)}) collective-permute-start(f32[4,128,128]{2,1,0:T(8,128)S(1)} %collective-permute-done.1.refs_3_), channel_id=1, source_target_pairs={{2,0},{4,2},{6,4},{8,6},{10,8},{12,10},{14,12},{16,14},{18,16},{20... | collective-permute-start | bytes 786440 | tf_op jit(solution)/shard_map/ppermute | solution.py:23
  14.1 1.1 %cosine_bitcast_fusion = (f32[1,128,128]{2,1,0:T(8,128)S(1)}, f32[1,128,128]{2,1,0:T(8,128)S(1)}) fusion(f32[128,128]{1,0:T(8,128)} %param.10), kind=kLoop, calls=%fused_computation.2 | loop fusion | bytes 196608 | tf_op jit(solution)/shard_map/stack | solution.py:360
  16.8 1.2 %collective-permute-done.3.refs_5_ = f32[4,128,128]{2,1,0:T(8,128)S(1)} collective-permute-done((f32[4,128,128]{2,1,0:T(8,128)S(1)}, f32[4,128,128]{2,1,0:T(8,128)S(1)}, u32[]{:S(2)}, u32[]{:S(2)}) %collective-permute-start.3) | collective-permute-done | bytes 262176 | tf_op jit(solution)/shard_map/ppermute | solution.py:23
  18.0 6.3 %shard_map.82 = (f32[2,256,256]{2,1,0:T(8,128)S(1)}, f32[2,128,256]{2,1,0:T(8,128)S(1)}, f32[2,128,128]{2,1,0:T(8,128)S(1)}, f32[2,128,128]{2,1,0:T(8,128)S(1)},...) custom-call(s32[13]{0:T(128)S(1)} %pad_add_fusion.refs_0_.scalar_ref, f32[2,2,256,256]{3,2,1,0:T(8,128)S(1)} %copy-done, ...), custom_call_target="tpu_custom_call" | custom-call | tf_op jit(solution)/shard_map/pallas_call | solution.py:315
  24.3 3.9 %shard_map.83 = (f32[2,256,256]{2,1,0:T(8,128)S(1)}, f32[4,128,256]{2,1,0:T(8,128)S(1)}, f32[2,128,128]{2,1,0:T(8,128)S(1)}, f32[2,128,128]{2,1,0:T(8,128)S(1)}, f32[2,128,128]{2,1,0:T(8,128)S(1)}) custom-call(s32[13]{0:T(128)S(1)} %pad_add_fusion.refs_0_.scalar_ref, f32[4,2,128,128]{3,2,1,0:T(8,128)S(1)} %get-tuple-element.39.back_ref, ...), custom_call_target="tpu_custom_call" | custom-call | tf_op jit(solution)/shard_map/pallas_call | solution.py:315
  28.5 1.2 %collective-permute-start.5 = (f32[2,128,128]{2,1,0:T(8,128)S(1)}, f32[2,128,128]{2,1,0:T(8,128)S(1)}, u32[]{:S(2)}, u32[]{:S(2)}) collective-permute-start(f32[2,128,128]{2,1,0:T(8,128)S(1)} %get-tuple-element.44), channel_id=1, source_target_pairs={{30,0},{0,2},{2,4},{4,6},{6,8},{8,10},{10,12},{12,14},{14,16},{16,... | collective-permute-start | bytes 393224 | tf_op jit(solution)/shard_map/ppermute | solution.py:23
  29.7 1.5 %collective-permute-start.10 = (f32[2,128,128]{2,1,0:T(8,128)S(1)}, f32[2,128,128]{2,1,0:T(8,128)S(1)}, u32[]{:S(2)}, u32[]{:S(2)}) collective-permute-start(f32[2,128,128]{2,1,0:T(8,128)S(1)} %get-tuple-element.49), channel_id=1, source_target_pairs={{1,0},{0,1},{3,2},{2,3},{5,4},{4,5},{7,6},{6,7},{9,8},{8,9},{11,10... | collective-permute-start | bytes 393224 | tf_op jit(solution)/shard_map/ppermute | solution.py:23
  31.2 9.9 %collective-permute-done.8 = f32[2,128,128]{2,1,0:T(8,128)S(1)} collective-permute-done((f32[2,128,128]{2,1,0:T(8,128)S(1)}, f32[2,128,128]{2,1,0:T(8,128)S(1)}, u32[]{:S(2)}, u32[]{:S(2)}) %collective-permute-start.8) | collective-permute-done | bytes 131104 | tf_op jit(solution)/shard_map/ppermute | solution.py:23
  41.2 1.6 %collective-permute-start.9 = (f32[2,128,128]{2,1,0:T(8,128)S(1)}, f32[2,128,128]{2,1,0:T(8,128)S(1)}, u32[]{:S(2)}, u32[]{:S(2)}) collective-permute-start(f32[2,128,128]{2,1,0:T(8,128)S(1)} %add.13), channel_id=1, source_target_pairs={{1,0},{0,1},{3,2},{2,3},{5,4},{4,5},{7,6},{6,7},{9,8},{8,9},{11,10... | collective-permute-start | bytes 393224 | tf_op jit(solution)/shard_map/ppermute | solution.py:23
  43.3 1.6 %collective-permute-start.6 = (f32[2,128,128]{2,1,0:T(8,128)S(1)}, f32[2,128,128]{2,1,0:T(8,128)S(1)}, u32[]{:S(2)}, u32[]{:S(2)}) collective-permute-start(f32[2,128,128]{2,1,0:T(8,128)S(1)} %add.12), channel_id=1, source_target_pairs={{1,0},{0,1},{3,2},{2,3},{5,4},{4,5},{7,6},{6,7},{9,8},{8,9},{11,10... | collective-permute-start | bytes 393224 | tf_op jit(solution)/shard_map/ppermute | solution.py:23
  44.9 1.3 %collective-permute-done.9.upper_ref = f32[2,128,128]{2,1,0:T(8,128)S(1)} collective-permute-done((f32[2,128,128]{2,1,0:T(8,128)S(1)}, f32[2,128,128]{2,1,0:T(8,128)S(1)}, u32[]{:S(2)}, u32[]{:S(2)}) %collective-permute-start.9) | collective-permute-done | bytes 131104 | tf_op jit(solution)/shard_map/ppermute | solution.py:23
  46.3 1.4 %collective-permute-done.7.lower_ref = f32[2,128,128]{2,1,0:T(8,128)S(1)} collective-permute-done((f32[2,128,128]{2,1,0:T(8,128)S(1)}, f32[2,128,128]{2,1,0:T(8,128)S(1)}, u32[]{:S(2)}, u32[]{:S(2)}) %collective-permute-start.7) | collective-permute-done | bytes 131104 | tf_op jit(solution)/shard_map/ppermute | solution.py:23
  47.7 1.4 %collective-permute-done.6.upper_ref = f32[2,128,128]{2,1,0:T(8,128)S(1)} collective-permute-done((f32[2,128,128]{2,1,0:T(8,128)S(1)}, f32[2,128,128]{2,1,0:T(8,128)S(1)}, u32[]{:S(2)}, u32[]{:S(2)}) %collective-permute-start.6) | collective-permute-done | bytes 131104 | tf_op jit(solution)/shard_map/ppermute | solution.py:23
  50.2 1.6 %collective-permute-start.12 = (f32[2,128,128]{2,1,0:T(8,128)S(1)}, f32[2,128,128]{2,1,0:T(8,128)S(1)}, u32[]{:S(2)}, u32[]{:S(2)}) collective-permute-start(f32[2,128,128]{2,1,0:T(8,128)S(1)} %get-tuple-element.53), channel_id=1, source_target_pairs={{1,0},{0,1},{3,2},{2,3},{5,4},{4,5},{7,6},{6,7},{9,8},{8,9},{11,10... | collective-permute-start | bytes 393224 | tf_op jit(solution)/shard_map/ppermute | solution.py:23
  52.2 1.6 %collective-permute-start.14 = (f32[4,128,128]{2,1,0:T(8,128)S(1)}, f32[4,128,128]{2,1,0:T(8,128)S(1)}, u32[]{:S(2)}, u32[]{:S(2)}) collective-permute-start(f32[4,128,128]{2,1,0:T(8,128)S(1)} %get-tuple-element.55), channel_id=1, source_target_pairs={{1,0},{0,1},{3,2},{2,3},{5,4},{4,5},{7,6},{6,7},{9,8},{8,9},{11,10... | collective-permute-start | bytes 786440 | tf_op jit(solution)/shard_map/ppermute | solution.py:23
  53.8 2.8 %collective-permute-done.12.refs_4_ = f32[2,128,128]{2,1,0:T(8,128)S(1)} collective-permute-done((f32[2,128,128]{2,1,0:T(8,128)S(1)}, f32[2,128,128]{2,1,0:T(8,128)S(1)}, u32[]{:S(2)}, u32[]{:S(2)}) %collective-permute-start.12) | collective-permute-done | bytes 131104 | tf_op jit(solution)/shard_map/ppermute | solution.py:23
  57.2 2.2 %collective-permute-done.13.refs_5_ = f32[2,128,128]{2,1,0:T(8,128)S(1)} collective-permute-done((f32[2,128,128]{2,1,0:T(8,128)S(1)}, f32[2,128,128]{2,1,0:T(8,128)S(1)}, u32[]{:S(2)}, u32[]{:S(2)}) %collective-permute-start.13) | collective-permute-done | bytes 131104 | tf_op jit(solution)/shard_map/ppermute | solution.py:23
  60.0 2.5 %collective-permute-done.16.refs_8_ = f32[2,128,128]{2,1,0:T(8,128)S(1)} collective-permute-done((f32[2,128,128]{2,1,0:T(8,128)S(1)}, f32[2,128,128]{2,1,0:T(8,128)S(1)}, u32[]{:S(2)}, u32[]{:S(2)}) %collective-permute-start.16) | collective-permute-done | bytes 131104 | tf_op jit(solution)/shard_map/ppermute | solution.py:23
  62.5 1.1 %collective-permute-done.14.refs_6_ = f32[4,128,128]{2,1,0:T(8,128)S(1)} collective-permute-done((f32[4,128,128]{2,1,0:T(8,128)S(1)}, f32[4,128,128]{2,1,0:T(8,128)S(1)}, u32[]{:S(2)}, u32[]{:S(2)}) %collective-permute-start.14) | collective-permute-done | bytes 262176 | tf_op jit(solution)/shard_map/ppermute | solution.py:23
  63.7 6.3 %shard_map.86 = (f32[2,256,256]{2,1,0:T(8,128)S(1)}, f32[2,128,256]{2,1,0:T(8,128)S(1)}, f32[2,128,128]{2,1,0:T(8,128)S(1)}, f32[2,128,128]{2,1,0:T(8,128)S(1)},...) custom-call(s32[13]{0:T(128)S(1)} %pad_add_fusion.refs_0_.scalar_ref, ...), custom_call_target="tpu_custom_call" | custom-call | tf_op jit(solution)/shard_map/pallas_call | solution.py:315
  70.0 3.9 %shard_map.87 = (f32[2,256,256]{2,1,0:T(8,128)S(1)}, f32[4,128,256]{2,1,0:T(8,128)S(1)}, f32[2,128,128]{2,1,0:T(8,128)S(1)}, f32[2,128,128]{2,1,0:T(8,128)S(1)}, f32[2,128,128]{2,1,0:T(8,128)S(1)}) custom-call(s32[13]{0:T(128)S(1)} %pad_add_fusion.refs_0_.scalar_ref, f32[4,2,128,128]{3,2,1,0:T(8,128)S(1)} %get-tuple-element.56.back_ref, ...), custom_call_target="tpu_custom_call" | custom-call | tf_op jit(solution)/shard_map/pallas_call | solution.py:315
  74.1 1.5 %collective-permute-start.23 = (f32[2,128,128]{2,1,0:T(8,128)S(1)}, f32[2,128,128]{2,1,0:T(8,128)S(1)}, u32[]{:S(2)}, u32[]{:S(2)}) collective-permute-start(f32[2,128,128]{2,1,0:T(8,128)S(1)} %get-tuple-element.66), channel_id=1, source_target_pairs={{1,0},{0,1},{3,2},{2,3},{5,4},{4,5},{7,6},{6,7},{9,8},{8,9},{11,10... | collective-permute-start | bytes 393224 | tf_op jit(solution)/shard_map/ppermute | solution.py:23
  76.2 10.5 %collective-permute-done.20 = f32[2,128,128]{2,1,0:T(8,128)S(1)} collective-permute-done((f32[2,128,128]{2,1,0:T(8,128)S(1)}, f32[2,128,128]{2,1,0:T(8,128)S(1)}, u32[]{:S(2)}, u32[]{:S(2)}) %collective-permute-start.20) | collective-permute-done | bytes 131104 | tf_op jit(solution)/shard_map/ppermute | solution.py:23
  86.7 1.5 %collective-permute-start.21 = (f32[2,128,128]{2,1,0:T(8,128)S(1)}, f32[2,128,128]{2,1,0:T(8,128)S(1)}, u32[]{:S(2)}, u32[]{:S(2)}) collective-permute-start(f32[2,128,128]{2,1,0:T(8,128)S(1)} %add.15), channel_id=1, source_target_pairs={{1,0},{0,1},{3,2},{2,3},{5,4},{4,5},{7,6},{6,7},{9,8},{8,9},{11,10... | collective-permute-start | bytes 393224 | tf_op jit(solution)/shard_map/ppermute | solution.py:23
  88.2 1.4 %collective-permute-start.19 = (f32[2,128,128]{2,1,0:T(8,128)S(1)}, f32[2,128,128]{2,1,0:T(8,128)S(1)}, u32[]{:S(2)}, u32[]{:S(2)}) collective-permute-start(f32[2,128,128]{2,1,0:T(8,128)S(1)} %add.14), channel_id=1, source_target_pairs={{1,0},{0,1},{3,2},{2,3},{5,4},{4,5},{7,6},{6,7},{9,8},{8,9},{11,10... | collective-permute-start | bytes 393224 | tf_op jit(solution)/shard_map/ppermute | solution.py:23
  89.6 2.2 %collective-permute-done.21.up_two = f32[2,128,128]{2,1,0:T(8,128)S(1)} collective-permute-done((f32[2,128,128]{2,1,0:T(8,128)S(1)}, f32[2,128,128]{2,1,0:T(8,128)S(1)}, u32[]{:S(2)}, u32[]{:S(2)}) %collective-permute-start.21) | collective-permute-done | bytes 131104 | tf_op jit(solution)/shard_map/ppermute | solution.py:23
  91.7 1.5 %collective-permute-done.19.up_one = f32[2,128,128]{2,1,0:T(8,128)S(1)} collective-permute-done((f32[2,128,128]{2,1,0:T(8,128)S(1)}, f32[2,128,128]{2,1,0:T(8,128)S(1)}, u32[]{:S(2)}, u32[]{:S(2)}) %collective-permute-start.19) | collective-permute-done | bytes 131104 | tf_op jit(solution)/shard_map/ppermute | solution.py:23
  93.2 1.2 %shard_map.88 = f32[2,2,256,256]{3,2,1,0:T(8,128)} custom-call(f32[2,256,256]{2,1,0:T(8,128)S(1)} %get-tuple-element.51.refs_1_.first_ref, f32[2,256,256]{2,1,0:T(8,128)S(1)} %get-tuple-element.50.second_ref.refs_2_, f32[2,256,256]{2,1,0:T(8,128)S(1)} %get-tuple-element.58.own_one, f32[2,256,256]{2,1,0:T(8,128)S(1)} %get-tuple-element.59.own_two, ...), custom_call_target="tpu_custom_call" | custom-call | tf_op jit(solution)/shard_map/pallas_call | solution.py:315
  (39 shorter events, 6.0 us)
Async XLA Ops:
  0.0 18.0 %copy-start = (f32[2,2,256,256]{3,2,1,0:T(8,128)S(1)}, f32[2,2,256,256]{3,2,1,0:T(8,128)}, u32[]{:S(2)}) copy-start(f32[2,2,256,256]{3,2,1,0:T(8,128)} %tile_ref.3) | copy-start | bytes 3145732
  1.4 10.2 %collective-permute-start.1 = (f32[4,128,128]{2,1,0:T(8,128)S(1)}, f32[4,128,128]{2,1,0:T(8,128)S(1)}, u32[]{:S(2)}, u32[]{:S(2)}) collective-permute-start(f32[4,128,128]{2,1,0:T(8,128)S(1)} %get-tuple-element.37), channel_id=1, source_target_pairs={{1,0},{0,1},{3,2},{2,3},{5,4},{4,5},{7,6},{6,7},{9,8},{8,9},{11,10... | collective-permute-start | bytes 786440 | tf_op jit(solution)/shard_map/ppermute | solution.py:23
  4.4 13.6 %collective-permute-start = (f32[4,128,256]{2,1,0:T(8,128)S(1)}, f32[4,128,256]{2,1,0:T(8,128)S(1)}, u32[]{:S(2)}, u32[]{:S(2)}) collective-permute-start(f32[4,128,256]{2,1,0:T(8,128)S(1)} %get-tuple-element.36), channel_id=1, source_target_pairs={{2,0},{4,2},{6,4},{8,6},{10,8},{12,10},{14,12},{16,14},{18,16},{20... | collective-permute-start | bytes 1572872 | tf_op jit(solution)/shard_map/ppermute | solution.py:23
  8.1 8.7 %collective-permute-start.2 = (f32[4,128,128]{2,1,0:T(8,128)S(1)}, f32[4,128,128]{2,1,0:T(8,128)S(1)}, u32[]{:S(2)}, u32[]{:S(2)}) collective-permute-start(f32[4,128,128]{2,1,0:T(8,128)S(1)} %get-tuple-element.38), channel_id=1, source_target_pairs={{1,0},{0,1},{3,2},{2,3},{5,4},{4,5},{7,6},{6,7},{9,8},{8,9},{11,10... | collective-permute-start | bytes 786440 | tf_op jit(solution)/shard_map/ppermute | solution.py:23
  11.6 6.4 %collective-permute-start.3 = (f32[4,128,128]{2,1,0:T(8,128)S(1)}, f32[4,128,128]{2,1,0:T(8,128)S(1)}, u32[]{:S(2)}, u32[]{:S(2)}) collective-permute-start(f32[4,128,128]{2,1,0:T(8,128)S(1)} %collective-permute-done.1.refs_3_), channel_id=1, source_target_pairs={{2,0},{4,2},{6,4},{8,6},{10,8},{12,10},{14,12},{16,14},{18,16},{20... | collective-permute-start | bytes 786440 | tf_op jit(solution)/shard_map/ppermute | solution.py:23
  15.2 0.7 copy-start.1
  16.1 0.7 copy-start.2
  28.3 17.9 %collective-permute-start.4 = (f32[4,128,256]{2,1,0:T(8,128)S(1)}, f32[4,128,256]{2,1,0:T(8,128)S(1)}, u32[]{:S(2)}, u32[]{:S(2)}) collective-permute-start(f32[4,128,256]{2,1,0:T(8,128)S(1)} %get-tuple-element.42), channel_id=1, source_target_pairs={{30,0},{0,2},{2,4},{4,6},{6,8},{8,10},{10,12},{12,14},{14,16},{16,... | collective-permute-start | bytes 1572872 | tf_op jit(solution)/shard_map/ppermute | solution.py:23
  28.3 12.8 %collective-permute-start.8 = (f32[2,128,128]{2,1,0:T(8,128)S(1)}, f32[2,128,128]{2,1,0:T(8,128)S(1)}, u32[]{:S(2)}, u32[]{:S(2)}) collective-permute-start(f32[2,128,128]{2,1,0:T(8,128)S(1)} %get-tuple-element.48), channel_id=1, source_target_pairs={{30,0},{0,2},{2,4},{4,6},{6,8},{8,10},{10,12},{12,14},{14,16},{16,... | collective-permute-start | bytes 393224 | tf_op jit(solution)/shard_map/ppermute | solution.py:23
  28.5 14.7 %collective-permute-start.5 = (f32[2,128,128]{2,1,0:T(8,128)S(1)}, f32[2,128,128]{2,1,0:T(8,128)S(1)}, u32[]{:S(2)}, u32[]{:S(2)}) collective-permute-start(f32[2,128,128]{2,1,0:T(8,128)S(1)} %get-tuple-element.44), channel_id=1, source_target_pairs={{30,0},{0,2},{2,4},{4,6},{6,8},{8,10},{10,12},{12,14},{14,16},{16,... | collective-permute-start | bytes 393224 | tf_op jit(solution)/shard_map/ppermute | solution.py:23
  29.7 15.2 %collective-permute-start.10 = (f32[2,128,128]{2,1,0:T(8,128)S(1)}, f32[2,128,128]{2,1,0:T(8,128)S(1)}, u32[]{:S(2)}, u32[]{:S(2)}) collective-permute-start(f32[2,128,128]{2,1,0:T(8,128)S(1)} %get-tuple-element.49), channel_id=1, source_target_pairs={{1,0},{0,1},{3,2},{2,3},{5,4},{4,5},{7,6},{6,7},{9,8},{8,9},{11,10... | collective-permute-start | bytes 393224 | tf_op jit(solution)/shard_map/ppermute | solution.py:23
  41.2 5.0 %collective-permute-start.9 = (f32[2,128,128]{2,1,0:T(8,128)S(1)}, f32[2,128,128]{2,1,0:T(8,128)S(1)}, u32[]{:S(2)}, u32[]{:S(2)}) collective-permute-start(f32[2,128,128]{2,1,0:T(8,128)S(1)} %add.13), channel_id=1, source_target_pairs={{1,0},{0,1},{3,2},{2,3},{5,4},{4,5},{7,6},{6,7},{9,8},{8,9},{11,10... | collective-permute-start | bytes 393224 | tf_op jit(solution)/shard_map/ppermute | solution.py:23
  42.8 5.0 %collective-permute-start.7 = (f32[2,128,128]{2,1,0:T(8,128)S(1)}, f32[2,128,128]{2,1,0:T(8,128)S(1)}, u32[]{:S(2)}, u32[]{:S(2)}) collective-permute-start(f32[2,128,128]{2,1,0:T(8,128)S(1)} %get-tuple-element.45), channel_id=1, source_target_pairs={{1,0},{0,1},{3,2},{2,3},{5,4},{4,5},{7,6},{6,7},{9,8},{8,9},{11,10... | collective-permute-start | bytes 393224 | tf_op jit(solution)/shard_map/ppermute | solution.py:23
  43.3 5.9 %collective-permute-start.6 = (f32[2,128,128]{2,1,0:T(8,128)S(1)}, f32[2,128,128]{2,1,0:T(8,128)S(1)}, u32[]{:S(2)}, u32[]{:S(2)}) collective-permute-start(f32[2,128,128]{2,1,0:T(8,128)S(1)} %add.12), channel_id=1, source_target_pairs={{1,0},{0,1},{3,2},{2,3},{5,4},{4,5},{7,6},{6,7},{9,8},{8,9},{11,10... | collective-permute-start | bytes 393224 | tf_op jit(solution)/shard_map/ppermute | solution.py:23
  49.3 14.4 %collective-permute-start.11 = (f32[4,128,256]{2,1,0:T(8,128)S(1)}, f32[4,128,256]{2,1,0:T(8,128)S(1)}, u32[]{:S(2)}, u32[]{:S(2)}) collective-permute-start(f32[4,128,256]{2,1,0:T(8,128)S(1)} %get-tuple-element.52), channel_id=1, source_target_pairs={{2,0},{4,2},{6,4},{8,6},{10,8},{12,10},{14,12},{16,14},{18,16},{20... | collective-permute-start | bytes 1572872 | tf_op jit(solution)/shard_map/ppermute | solution.py:23
  50.2 6.4 %collective-permute-start.12 = (f32[2,128,128]{2,1,0:T(8,128)S(1)}, f32[2,128,128]{2,1,0:T(8,128)S(1)}, u32[]{:S(2)}, u32[]{:S(2)}) collective-permute-start(f32[2,128,128]{2,1,0:T(8,128)S(1)} %get-tuple-element.53), channel_id=1, source_target_pairs={{1,0},{0,1},{3,2},{2,3},{5,4},{4,5},{7,6},{6,7},{9,8},{8,9},{11,10... | collective-permute-start | bytes 393224 | tf_op jit(solution)/shard_map/ppermute | solution.py:23
  51.8 7.6 %collective-permute-start.13 = (f32[2,128,128]{2,1,0:T(8,128)S(1)}, f32[2,128,128]{2,1,0:T(8,128)S(1)}, u32[]{:S(2)}, u32[]{:S(2)}) collective-permute-start(f32[2,128,128]{2,1,0:T(8,128)S(1)} %get-tuple-element.54), channel_id=1, source_target_pairs={{1,0},{0,1},{3,2},{2,3},{5,4},{4,5},{7,6},{6,7},{9,8},{8,9},{11,10... | collective-permute-start | bytes 393224 | tf_op jit(solution)/shard_map/ppermute | solution.py:23
  52.2 11.5 %collective-permute-start.14 = (f32[4,128,128]{2,1,0:T(8,128)S(1)}, f32[4,128,128]{2,1,0:T(8,128)S(1)}, u32[]{:S(2)}, u32[]{:S(2)}) collective-permute-start(f32[4,128,128]{2,1,0:T(8,128)S(1)} %get-tuple-element.55), channel_id=1, source_target_pairs={{1,0},{0,1},{3,2},{2,3},{5,4},{4,5},{7,6},{6,7},{9,8},{8,9},{11,10... | collective-permute-start | bytes 786440 | tf_op jit(solution)/shard_map/ppermute | solution.py:23
  56.6 3.4 %collective-permute-start.15 = (f32[2,128,128]{2,1,0:T(8,128)S(1)}, f32[2,128,128]{2,1,0:T(8,128)S(1)}, u32[]{:S(2)}, u32[]{:S(2)}) collective-permute-start(f32[2,128,128]{2,1,0:T(8,128)S(1)} %collective-permute-done.12.refs_4_), channel_id=1, source_target_pairs={{2,0},{4,2},{6,4},{8,6},{10,8},{12,10},{14,12},{16,14},{18,16},{20... | collective-permute-start | bytes 393224 | tf_op jit(solution)/shard_map/ppermute | solution.py:23
  59.4 3.2 %collective-permute-start.16 = (f32[2,128,128]{2,1,0:T(8,128)S(1)}, f32[2,128,128]{2,1,0:T(8,128)S(1)}, u32[]{:S(2)}, u32[]{:S(2)}) collective-permute-start(f32[2,128,128]{2,1,0:T(8,128)S(1)} %collective-permute-done.13.refs_5_), channel_id=1, source_target_pairs={{2,0},{4,2},{6,4},{8,6},{10,8},{12,10},{14,12},{16,14},{18,16},{20... | collective-permute-start | bytes 393224 | tf_op jit(solution)/shard_map/ppermute | solution.py:23
  73.9 19.3 %collective-permute-start.17 = (f32[4,128,256]{2,1,0:T(8,128)S(1)}, f32[4,128,256]{2,1,0:T(8,128)S(1)}, u32[]{:S(2)}, u32[]{:S(2)}) collective-permute-start(f32[4,128,256]{2,1,0:T(8,128)S(1)} %get-tuple-element.60), channel_id=1, source_target_pairs={{30,0},{0,2},{2,4},{4,6},{6,8},{8,10},{10,12},{12,14},{14,16},{16,... | collective-permute-start | bytes 1572872 | tf_op jit(solution)/shard_map/ppermute | solution.py:23
  74.0 12.7 %collective-permute-start.20 = (f32[2,128,128]{2,1,0:T(8,128)S(1)}, f32[2,128,128]{2,1,0:T(8,128)S(1)}, u32[]{:S(2)}, u32[]{:S(2)}) collective-permute-start(f32[2,128,128]{2,1,0:T(8,128)S(1)} %get-tuple-element.64), channel_id=1, source_target_pairs={{30,0},{0,2},{2,4},{4,6},{6,8},{8,10},{10,12},{12,14},{14,16},{16,... | collective-permute-start | bytes 393224 | tf_op jit(solution)/shard_map/ppermute | solution.py:23
  74.1 14.1 %collective-permute-start.18 = (f32[2,128,128]{2,1,0:T(8,128)S(1)}, f32[2,128,128]{2,1,0:T(8,128)S(1)}, u32[]{:S(2)}, u32[]{:S(2)}) collective-permute-start(f32[2,128,128]{2,1,0:T(8,128)S(1)} %get-tuple-element.62), channel_id=1, source_target_pairs={{30,0},{0,2},{2,4},{4,6},{6,8},{8,10},{10,12},{12,14},{14,16},{16,... | collective-permute-start | bytes 393224 | tf_op jit(solution)/shard_map/ppermute | solution.py:23
  74.1 15.5 %collective-permute-start.23 = (f32[2,128,128]{2,1,0:T(8,128)S(1)}, f32[2,128,128]{2,1,0:T(8,128)S(1)}, u32[]{:S(2)}, u32[]{:S(2)}) collective-permute-start(f32[2,128,128]{2,1,0:T(8,128)S(1)} %get-tuple-element.66), channel_id=1, source_target_pairs={{1,0},{0,1},{3,2},{2,3},{5,4},{4,5},{7,6},{6,7},{9,8},{8,9},{11,10... | collective-permute-start | bytes 393224 | tf_op jit(solution)/shard_map/ppermute | solution.py:23
  75.6 14.0 %collective-permute-start.22 = (f32[2,128,128]{2,1,0:T(8,128)S(1)}, f32[2,128,128]{2,1,0:T(8,128)S(1)}, u32[]{:S(2)}, u32[]{:S(2)}) collective-permute-start(f32[2,128,128]{2,1,0:T(8,128)S(1)} %get-tuple-element.65), channel_id=1, source_target_pairs={{1,0},{0,1},{3,2},{2,3},{5,4},{4,5},{7,6},{6,7},{9,8},{8,9},{11,10... | collective-permute-start | bytes 393224 | tf_op jit(solution)/shard_map/ppermute | solution.py:23
  86.7 5.0 %collective-permute-start.21 = (f32[2,128,128]{2,1,0:T(8,128)S(1)}, f32[2,128,128]{2,1,0:T(8,128)S(1)}, u32[]{:S(2)}, u32[]{:S(2)}) collective-permute-start(f32[2,128,128]{2,1,0:T(8,128)S(1)} %add.15), channel_id=1, source_target_pairs={{1,0},{0,1},{3,2},{2,3},{5,4},{4,5},{7,6},{6,7},{9,8},{8,9},{11,10... | collective-permute-start | bytes 393224 | tf_op jit(solution)/shard_map/ppermute | solution.py:23
  88.2 5.0 %collective-permute-start.19 = (f32[2,128,128]{2,1,0:T(8,128)S(1)}, f32[2,128,128]{2,1,0:T(8,128)S(1)}, u32[]{:S(2)}, u32[]{:S(2)}) collective-permute-start(f32[2,128,128]{2,1,0:T(8,128)S(1)} %add.14), channel_id=1, source_target_pairs={{1,0},{0,1},{3,2},{2,3},{5,4},{4,5},{7,6},{6,7},{9,8},{8,9},{11,10... | collective-permute-start | bytes 393224 | tf_op jit(solution)/shard_map/ppermute | solution.py:23
